TPU v7x, 32 devices: a whole 2x2x4 slice. The times are simulated.
32 devices in a mesh: order: 8 (over z, x), chan: 4 (over y, core).
Axes of the slice: x: 2, y: 2, z: 4, core: 2. Of those that a mesh axis runs over, the one named last changes fastest.
Arguments:
- cotangent: bfloat16 [248, 240, 1, 2, 1024], P('order', None, None, None, 'chan'), may hold values from -0.59765625 to 0.59765625
- stored_coefficients: bfloat16 [248, 240, 1, 2, 1024], P('order', None, None, None, 'chan'), may hold values from -0.29882812 to 0.29882812
- weights: bfloat16 [248, 1024, 1024], P('order', 'chan'), may hold values from -0.1875 to 0.1875
- order_table: int32 [248], replicated, may hold values from 0 to 240, as said below
- degree_table: int32 [248], replicated, may hold values from 0 to 240, as said below
Outputs:
- input_gradient: bfloat16 [248, 240, 1, 2, 1024], P('order', None, None, None, 'chan')
- mixing_gradient: bfloat16 [248, 1024, 1024], P('order', 'chan')
Inputs may be any that keep to these rules, and one draw needn't show every extreme that they name: `order_table`: each order 0 to 239 stands in exactly one slot; every other slot holds 240, meaning empty. `degree_table`: each degree 0 to 239 stands in exactly one slot; every other slot holds 240, meaning empty.
All inputs are finite; a program needn't handle non-finite values.
Results may differ from a plain program's by a relative error of at most 0.008.
Values may be sent and summed in bfloat16 or wider, within the bound.
A program may use at most 192 MiB of HBM per device.

v0:
```python
import jax
import jax.numpy as jnp
from jax import lax
from jax.sharding import PartitionSpec as P


def legendre_rows(orders, degree_range, latitude_count):
    order_real = orders.astype(jnp.float32)[:, None]
    angles = jnp.pi * (jnp.arange(latitude_count).astype(jnp.float32) + 0.5) / latitude_count
    cosine = jnp.cos(angles)[None, :]
    sine = jnp.sin(angles)[None, :]
    counter = jnp.arange(1, degree_range + 1).astype(jnp.float32)
    factors = jnp.log((2.0 * counter - 1.0) / (2.0 * counter))
    below = (counter[None, :] <= order_real).astype(jnp.float32)
    log_start = 0.5 * (
        jnp.log((2.0 * order_real + 1.0) / (4.0 * jnp.pi))
        + jnp.sum(below * factors[None, :], axis=1, keepdims=True)
    )
    parity = 1.0 - 2.0 * (orders % 2).astype(jnp.float32)[:, None]
    start = parity * jnp.exp(log_start + order_real * jnp.log(sine))

    def advance(carry, degree):
        latest, before = carry
        level = degree.astype(jnp.float32)
        upper = jnp.sqrt(
            jnp.maximum(4.0 * level * level - 1.0, 0.0)
            / jnp.maximum(level * level - order_real * order_real, 1.0)
        )
        lower = jnp.sqrt(
            jnp.maximum((level - 1.0) * (level - 1.0) - order_real * order_real, 0.0)
            / jnp.maximum(4.0 * (level - 1.0) * (level - 1.0) - 1.0, 1.0)
        )
        grown = upper * (cosine * latest - lower * before)
        fresh = jnp.where(
            level == order_real, start, jnp.where(level > order_real, grown, jnp.zeros_like(grown))
        )
        return ((fresh, latest), fresh)

    zeros = jnp.zeros((orders.shape[0], latitude_count), jnp.float32)
    unused_result, stacked = lax.scan(advance, (zeros, zeros), jnp.arange(degree_range))
    return jnp.transpose(stacked, (1, 0, 2))


def quadrature(latitude_count):
    angles = jnp.pi * (jnp.arange(latitude_count).astype(jnp.float32) + 0.5) / latitude_count
    return jnp.pi / latitude_count * jnp.sin(angles)


def per_device(cotangent, stored_coefficients, weights, order_table, degree_table):
    slots, latitude_count, batch_size, unused_result, slot_width = cotangent.shape
    degree_range = stored_coefficients.shape[1]
    peers = lax.axis_size("order")
    position = lax.axis_index("order")
    mine = lax.dynamic_slice_in_dim(order_table, position * slots, slots)
    table = legendre_rows(mine, degree_range, latitude_count)
    table_halfprecision = table.astype(jnp.bfloat16)
    flat_cotangent = cotangent.reshape(slots, latitude_count, batch_size * 2 * slot_width)
    adjoint = jnp.einsum(
        "slj,sjf->slf", table_halfprecision, flat_cotangent, preferred_element_type=jnp.float32
    ).astype(jnp.bfloat16)
    adjoint = adjoint.reshape(slots, degree_range, batch_size * 2, slot_width)
    active_mask = jnp.arange(degree_range)[None, :] >= mine[:, None]
    masked_values = stored_coefficients.reshape(
        slots, degree_range, batch_size * 2, slot_width
    ) * active_mask[:, :, None, None].astype(jnp.bfloat16)
    clipped = jnp.minimum(degree_table, degree_range - 1)
    valid = (degree_table[None, :] >= mine[:, None]) & (degree_table[None, :] < degree_range)
    valid_bf = valid.astype(jnp.bfloat16)

    def pack_rows(source):
        picked = jnp.take(source, clipped, axis=1) * valid_bf[:, :, None, None]
        return picked.reshape(slots, peers, slots, batch_size * 2, source.shape[3])

    send_adjoint = pack_rows(adjoint)
    send_saved = pack_rows(masked_values)
    recv_saved, recv_adjoint = (
        lax.all_to_all(send_saved, "order", split_axis=1, concat_axis=1, tiled=True),
        lax.all_to_all(send_adjoint, "order", split_axis=1, concat_axis=1, tiled=True),
    )
    recv_adjoint = lax.all_gather(recv_adjoint, "chan", axis=4, tiled=True)
    mixing_gradient = jnp.einsum(
        "sntrc,sntrd->tcd", recv_saved, recv_adjoint, preferred_element_type=jnp.float32
    ).astype(jnp.bfloat16)
    coefficient_gradient = jnp.einsum(
        "sntrd,tcd->sntrc", recv_adjoint, weights, preferred_element_type=jnp.float32
    ).astype(jnp.bfloat16)
    returned = lax.all_to_all(
        coefficient_gradient, "order", split_axis=1, concat_axis=1, tiled=True
    )
    returned = returned.reshape(slots, peers * slots, batch_size * 2 * slot_width)
    picked_table = jnp.take(table_halfprecision, clipped, axis=1) * valid_bf[:, :, None]
    summed = jnp.einsum("skj,skf->sjf", picked_table, returned, preferred_element_type=jnp.float32)
    quad = quadrature(latitude_count)
    input_gradient = (summed * quad[None, :, None]).astype(jnp.bfloat16)
    return (
        input_gradient.reshape(slots, latitude_count, batch_size, 2, slot_width),
        mixing_gradient,
    )


def solution(mesh):
    return jax.shard_map(
        per_device,
        mesh=mesh,
        in_specs=(
            P("order", None, None, None, "chan"),
            P("order", None, None, None, "chan"),
            P("order", "chan", None),
            P(),
            P(),
        ),
        out_specs=(P("order", None, None, None, "chan"), P("order", "chan", None)),
        check_vma=False,
    )
```

profile of v0, /device:TPU:0, one launch (start us, length us, event | category | flops | bytes accessed | tf_op | source)
XLA Modules:
  0.0 1286.6 jit_solution(11286440266197965360)
XLA Ops:
  7.3 0.8 fusion.22
  9.7 491.0 %while.18 = (s32[]{:T(128)}, f32[31,240]{1,0:T(8,128)S(1)}, f32[31,240]{1,0:T(8,128)S(1)}, bf16[240,31,240]{2,1,0:T(8,128)(2,1)}, s32[240]{0:T(256)S(1)}, /*inde...) while((s32[]{:T(128)}, f32[31,240]{1,0:T(8,128)S(1)}, ...), condition=%wide.region_2.3_spmd.clone, body=%wide.region_1.2_spmd.clone.sunk | while | flops 75383 | bytes 156779 | solution.py:40
  15.2 0.7 bitcast_dynamic-update-slice_fusion.2
  31.5 0.7 bitcast_dynamic-update-slice_fusion.2
  35.6 0.7 bitcast_dynamic-update-slice_fusion.2
  47.9 0.7 bitcast_dynamic-update-slice_fusion.2
  64.3 0.7 bitcast_dynamic-update-slice_fusion.2
  86.8 0.7 bitcast_dynamic-update-slice_fusion.2
  95.0 0.7 bitcast_dynamic-update-slice_fusion.2
  113.4 0.7 bitcast_dynamic-update-slice_fusion.2
  121.6 0.7 bitcast_dynamic-update-slice_fusion.2
  135.9 0.7 bitcast_dynamic-update-slice_fusion.2
  154.3 0.7 bitcast_dynamic-update-slice_fusion.2
  160.4 0.7 bitcast_dynamic-update-slice_fusion.2
  162.5 0.7 bitcast_dynamic-update-slice_fusion.2
  170.7 0.7 bitcast_dynamic-update-slice_fusion.2
  176.8 0.7 bitcast_dynamic-update-slice_fusion.2
  195.2 0.7 bitcast_dynamic-update-slice_fusion.2
  201.4 0.7 bitcast_dynamic-update-slice_fusion.2
  209.5 0.7 bitcast_dynamic-update-slice_fusion.2
  234.1 0.7 bitcast_dynamic-update-slice_fusion.2
  244.3 0.7 bitcast_dynamic-update-slice_fusion.2
  275.0 0.7 bitcast_dynamic-update-slice_fusion.2
  277.1 0.7 bitcast_dynamic-update-slice_fusion.2
  283.2 0.7 bitcast_dynamic-update-slice_fusion.2
  309.8 0.7 bitcast_dynamic-update-slice_fusion.2
  356.8 0.7 bitcast_dynamic-update-slice_fusion.2
  360.9 0.7 bitcast_dynamic-update-slice_fusion.2
  365.0 0.7 bitcast_dynamic-update-slice_fusion.2
  367.1 0.7 bitcast_dynamic-update-slice_fusion.2
  381.4 0.7 bitcast_dynamic-update-slice_fusion.2
  391.6 0.7 bitcast_dynamic-update-slice_fusion.2
  424.4 0.7 bitcast_dynamic-update-slice_fusion.2
  430.5 0.7 bitcast_dynamic-update-slice_fusion.2
  440.7 0.7 bitcast_dynamic-update-slice_fusion.2
  448.9 0.7 bitcast_dynamic-update-slice_fusion.2
  455.1 0.7 bitcast_dynamic-update-slice_fusion.2
  463.2 0.7 bitcast_dynamic-update-slice_fusion.2
  467.3 0.7 bitcast_dynamic-update-slice_fusion.2
  471.4 0.7 bitcast_dynamic-update-slice_fusion.2
  479.6 0.7 bitcast_dynamic-update-slice_fusion.2
  496.0 0.7 bitcast_dynamic-update-slice_fusion.2
  500.8 17.3 %reshape.244 = bf16[31,240,512]{2,1,0:T(8,128)(2,1)} reshape(bf16[31,240,1,2,256]{4,3,2,1,0:T(2,128)(2,1)} %param.9) | data formatting | bytes 15237120 | tf_op jit(solution)/shard_map/reshape | solution.py:57
  518.1 12.3 convolution_convert_fusion
  530.4 16.2 %reshape.245 = bf16[31,240,2,256]{3,2,1,0:T(2,128)(2,1)} reshape(bf16[31,240,512]{2,1,0:T(8,128)(2,1)} %convolution_convert_fusion) | data formatting | bytes 15237120 | tf_op jit(solution)/shard_map/reshape | solution.py:61
  546.6 28.2 %gather_fusion.1 = bf16[248,31,2,256]{3,2,1,0:T(2,128)(2,1)} fusion(bf16[31,240,2,256]{3,2,1,0:T(2,128)(2,1)} %reshape.245, s32[1024]{0:T(1024)S(1)} %pad_clamp_fusion), kind=kCustom, calls=%fused_computation.clone | custom fusion | bytes 15746016 | tf_op jit(solution)/shard_map/jit(_take)/gather | solution.py:71
  574.7 11.6 bitcast_multiply_fusion.2
  586.3 28.5 %gather_fusion.2 = bf16[248,31,2,256]{3,2,1,0:T(2,128)(2,1)} fusion(bf16[31,240,2,256]{3,2,1,0:T(2,128)(2,1)} %bitcast_multiply_fusion.2, s32[1024]{0:T(1024)S(1)} %pad_clamp_fusion), kind=kCustom, calls=%fused_computation.1.clone | custom fusion | bytes 15746016 | tf_op jit(solution)/shard_map/jit(_take)/gather | solution.py:71
  615.0 20.7 %bitcast_multiply_fusion = (bf16[31,248,2,256]{3,2,0,1:T(2,128)(2,1)}, bf16[31,248,2,256]{3,2,0,1:T(2,128)(2,1)S(1)}) fusion(bf16[248,31,2,256]{3,2,1,0:T(2,128)(2,1)} %gather_fusion.2, pred[248]{0:T(512)(128)(4,1)S(1)} %get-tuple-element.223, bf16[31,248]{0,1:T(8,128)(2,1)S(1)} %and_convert_fusion, bf16[248,31,2,256]{3,2,1,0:T(2,128)(2,1)} %gather_fusion.1), kind=kLoop, calls=%fused_computation.22 | loop fusion | flops 15745024 | bytes 31505672 | tf_op jit(solution)/shard_map/mul | solution.py:71
  635.7 179.9 %all_to_all.15 = bf16[31,8,31,2,256]{4,3,0,2,1:T(2,128)(2,1)S(1)} all-to-all(bf16[31,8,31,2,256]{4,3,0,2,1:T(2,128)(2,1)S(1)} %bitcast.58), channel_id=1, replica_groups=mesh['order'=8,'chan'=4] {'order'}, dimensions={1} | all-to-all | bytes 15745024 | tf_op jit(solution)/shard_map/all_to_all | solution.py:78
  815.6 5.4 copy.23
  820.9 7.7 copy.28
  828.6 5.1 all-to-all-start.2
  833.8 6.8 gather_fusion
  841.1 6.0 bitcast_multiply_fusion.3
  847.1 166.1 %all-gather.2.cloned.1.call-done = bf16[31,8,31,2,1024]{4,1,3,0,2:T(8,128)(2,1)} async-done(((bf16[31,8,31,2,256]{4,1,3,0,2:T(8,128)(2,1)}), bf16[31,8,31,2,1024]{4,1,3,0,2:T(8,128)(2,1)}) %all-gather.2.cloned.1.call-update) | async-done | bytes 31490064 | tf_op jit(solution)/shard_map/all_gather | solution.py:80
  1013.3 19.7 %convert_bitcast_fusion = bf16[31,8,31,2,256]{4,1,3,0,2:T(8,128)(2,1)} fusion(bf16[31,8,31,2,1024]{4,1,3,0,2:T(8,128)(2,1)} %all-gather.2.cloned.1.call-done, bf16[31,256,1024]{2,1,0:T(8,128)(2,1)} %param.11), kind=kOutput, calls=%fused_computation.25 | convolution fusion | flops 8065388544 | bytes 55615488 | tf_op jit(solution)/shard_map/sntrd,tcd->sntrc/dot_general | solution.py:84
  1033.0 12.8 copy.24
  1045.8 5.5 all-to-all-start.1
  1051.3 23.4 %bitcast_convert_fusion = bf16[31,256,1024]{2,1,0:T(8,128)(2,1)} fusion(bf16[31,8,31,2,1024]{4,1,3,0,2:T(8,128)(2,1)} %all-gather.2.cloned.1.call-done, bf16[31,8,31,2,256]{4,3,2,0,1:T(2,128)(2,1)} %all-to-all-done.2), kind=kOutput, calls=%fused_computation.13 | convolution fusion | flops 8069578752 | bytes 55615488 | tf_op jit(solution)/shard_map/sntrc,sntrd->tcd/dot_general | solution.py:81
  1074.7 149.1 %all-to-all-done.1 = bf16[31,8,31,2,256]{4,3,0,2,1:T(2,128)(2,1)} async-done(((bf16[31,8,31,2,256]{4,3,0,2,1:T(2,128)(2,1)}), bf16[31,8,31,2,256]{4,3,0,2,1:T(2,128)(2,1)}, u32[]{:S(2)}, u32[]{:S(2)}) %all-to-all-start.1) | async-done | bytes 7872544 | tf_op jit(solution)/shard_map/all_to_all | solution.py:87
  1223.8 17.9 %reshape.284 = bf16[31,248,512]{2,0,1:T(8,128)(2,1)} reshape(bf16[31,8,31,2,256]{4,3,0,2,1:T(2,128)(2,1)} %all-to-all-done.1) | data formatting | bytes 15745024 | tf_op jit(solution)/shard_map/reshape | solution.py:90
  1241.8 21.5 %multiply_convert_fusion = bf16[31,240,512]{2,1,0:T(8,128)(2,1)} fusion(bf16[31,248,512]{2,0,1:T(8,128)(2,1)} %reshape.284, f32[240]{0:T(256)S(1)} %copy-done.1, bf16[31,248,240]{2,0,1:T(8,128)(2,1)} %bitcast_multiply_fusion.3), kind=kOutput, calls=%fused_computation.20 | convolution fusion | flops 1897021440 | bytes 19182272 | tf_op jit(solution)/shard_map/skj,skf->sjf/dot_general | solution.py:92
  1263.3 16.2 %reshape.248 = bf16[31,240,1,2,256]{4,3,1,0,2:T(2,128)(2,1)} reshape(bf16[31,240,512]{2,1,0:T(8,128)(2,1)} %multiply_convert_fusion) | data formatting | bytes 15237120 | tf_op jit(solution)/shard_map/reshape | solution.py:96
  (1183 shorter events, 301.0 us)
Async XLA Ops:
  7.2 1006.1 %all-gather.2.cloned.1.call-start = ((), (), s32[]{:S(2)}) async-start(), calls=%async_computation.3 | async-start | bytes 39362560 | tf_op jit(solution)/shard_map/all_gather | solution.py:80
  586.3 28.5 %copy-start = (s32[248]{0:T(256)S(1)}, s32[248]{0:T(256)}, u32[]{:S(2)}) copy-start(s32[248]{0:T(256)} %param.13) | copy-start | bytes 2980
  828.6 217.1 %all-to-all-start.2 = ((bf16[31,8,31,2,256]{4,3,2,0,1:T(2,128)(2,1)}), bf16[31,8,31,2,256]{4,3,2,0,1:T(2,128)(2,1)}, u32[]{:S(2)}, u32[]{:S(2)}) async-start(bf16[31,8,31,2,256]{4,3,2,0,1:T(2,128)(2,1)} %copy.28), calls=%async_computation.2 | async-start | bytes 15745024 | tf_op jit(solution)/shard_map/all_to_all | solution.py:77
  1045.8 178.0 %all-to-all-start.1 = ((bf16[31,8,31,2,256]{4,3,0,2,1:T(2,128)(2,1)}), bf16[31,8,31,2,256]{4,3,0,2,1:T(2,128)(2,1)}, u32[]{:S(2)}, u32[]{:S(2)}) async-start(bf16[31,8,31,2,256]{4,3,0,2,1:T(2,128)(2,1)} %copy.24), calls=%async_computation.1 | async-start | bytes 15745024 | tf_op jit(solution)/shard_map/all_to_all | solution.py:87
  1074.7 167.0 %copy-start.1 = (f32[240]{0:T(256)S(1)}, f32[240]{0:T(256)}, u32[]{:S(2)}) copy-start(f32[240]{0:T(256)} %fusion.18) | copy-start | bytes 2884
Sparse Core Ops, SparseCore 0:
  821.1 192.1 all-gather.1
where the time goes:
time: 1300 us; the launch traced here: 1290 us
  waiting for transfers between devices  315 us (24%)
  local copies, waits for them, and re-layouts  297 us (23%)
  other arithmetic  229 us (18%)
  blocking collectives  180 us (14%)
  loops' own time  164 us (13%)
  matrix products  76.9 us (6%)
  between operations  14.4 us (1%)
    all_to_all x1, blocking collectives, per_device(): lax.all_to_all(send_adjoint, 'order', split_axis=1, concat_axis=1, tiled=...  180 us
    dynamic_update_slice x240, other arithmetic, legendre_rows(): lax.scan(advance, (zeros, zeros), jnp.arange(degree_range))  169 us
    all_gather x1, waiting for transfers between devices, per_device(): recv_adjoint = lax.all_gather(recv_adjoint, 'chan', axis=4, tiled=True)  166 us
    another operation x1, loops' own time, legendre_rows(): lax.scan(advance, (zeros, zeros), jnp.arange(degree_range))  164 us
    all_to_all x1, waiting for transfers between devices, per_device(): lax.all_to_all(coefficient_gradient, 'order', split_axis=1, concat_axis=1...  149 us
    dynamic_slice x240, local copies, waits for them, and re-layouts, legendre_rows(): lax.scan(advance, (zeros, zeros), jnp.arange(degree_range))  140 us
    gather x2, local copies, waits for them, and re-layouts, pack_rows(): picked = jnp.take(source, clipped, axis=1) * valid_bf[:, :, None, None]  56.7 us
  transfers between devices with their start and end apart: 3, of which 2 were waited for; matrix products, arithmetic and copies ran while one was open for 6% of the time, Pallas kernels for 0%

commit v1 on v0

v1 whole, which is shorter than its diff:
```python
import functools

import jax
import jax.numpy as jnp
from jax import lax
from jax.experimental import pallas as pl
from jax.experimental.pallas import tpu as pltpu
from jax.sharding import PartitionSpec as P

CHUNKS = 2
LANES = 128


def recurrence_kernel(unroll, where_ref, upper_ref, lower_ref, order_ref, cosine_ref, start_ref, out_ref):
    degree_range = upper_ref.shape[0]
    latitude_count = out_ref.shape[2]
    pieces = [(lo, min(lo + LANES, latitude_count)) for lo in range(0, latitude_count, LANES)]
    out_ref[...] = jnp.zeros_like(out_ref)
    order = order_ref[...]
    cosine = [cosine_ref[:, lo:hi] for lo, hi in pieces]
    start = [start_ref[:, lo:hi] for lo, hi in pieces]

    def body(step, carry):
        latest, before = carry
        for inner in range(unroll):
            level = step * unroll + inner
            row = where_ref[level]
            upper = upper_ref[level]
            lower = lower_ref[level]
            begins = order == level
            fresh = []
            for i, (lo, hi) in enumerate(pieces):
                width = hi - lo
                grown = upper[:, :width] * (cosine[i] * latest[i] - lower[:, :width] * before[i])
                value = jnp.where(begins[:, :width], start[i], grown)
                out_ref[row, :, lo:hi] = value.astype(jnp.bfloat16)
                fresh.append(value)
            latest, before = fresh, latest
        return latest, before

    zeros = [jnp.zeros_like(c) for c in cosine]
    lax.fori_loop(0, degree_range // unroll, body, (zeros, zeros))


def picked_legendre(orders, degree_table, degree_range, latitude_count):
    slots = orders.shape[0]
    total = degree_table.shape[0]
    order_real = orders.astype(jnp.float32)[:, None]
    angles = jnp.pi * (jnp.arange(latitude_count).astype(jnp.float32) + 0.5) / latitude_count
    cosine = jnp.cos(angles)[None, :]
    sine = jnp.sin(angles)[None, :]
    counter = jnp.arange(1, degree_range + 1).astype(jnp.float32)
    factors = jnp.log((2.0 * counter - 1.0) / (2.0 * counter))
    below = (counter[None, :] <= order_real).astype(jnp.float32)
    log_start = 0.5 * (
        jnp.log((2.0 * order_real + 1.0) / (4.0 * jnp.pi))
        + jnp.sum(below * factors[None, :], axis=1, keepdims=True)
    )
    parity = 1.0 - 2.0 * (orders % 2).astype(jnp.float32)[:, None]
    start = parity * jnp.exp(log_start + order_real * jnp.log(sine))

    level = jnp.arange(degree_range).astype(jnp.float32)[:, None, None]
    order_wide = jnp.broadcast_to(order_real[None], (1, slots, LANES))
    upper = jnp.sqrt(
        jnp.maximum(4.0 * level * level - 1.0, 0.0)
        / jnp.maximum(level * level - order_wide * order_wide, 1.0)
    )
    lower = jnp.sqrt(
        jnp.maximum((level - 1.0) * (level - 1.0) - order_wide * order_wide, 0.0)
        / jnp.maximum(4.0 * (level - 1.0) * (level - 1.0) - 1.0, 1.0)
    )
    places = jnp.arange(total).astype(jnp.int32)
    degrees = jnp.arange(degree_range).astype(jnp.int32)
    where = jnp.sum(
        jnp.where(degree_table[None, :] == degrees[:, None], places[None, :], 0), axis=1
    )
    where = jnp.minimum(where, total - 1).astype(jnp.int32)
    unroll = next(u for u in (8, 6, 5, 4, 3, 2, 1) if degree_range % u == 0)
    vmem = pl.BlockSpec(memory_space=pltpu.VMEM)
    return pl.pallas_call(
        functools.partial(recurrence_kernel, unroll),
        out_shape=jax.ShapeDtypeStruct((total, slots, latitude_count), jnp.bfloat16),
        in_specs=[pl.BlockSpec(memory_space=pltpu.SMEM)] + [vmem] * 5,
        out_specs=vmem,
        cost_estimate=pl.CostEstimate(
            flops=6 * degree_range * slots * latitude_count,
            bytes_accessed=24 * 1024 * 1024,
            transcendentals=0,
        ),
        name="legendre",
    )(
        where,
        upper,
        lower,
        jnp.broadcast_to(orders[:, None], (slots, LANES)),
        jnp.broadcast_to(cosine, (slots, latitude_count)),
        start,
    )


def quadrature(latitude_count):
    angles = jnp.pi * (jnp.arange(latitude_count).astype(jnp.float32) + 0.5) / latitude_count
    return jnp.pi / latitude_count * jnp.sin(angles)


def per_device(cotangent, stored_coefficients, weights, order_table, degree_table):
    slots, latitude_count, batch_size, parts, width = cotangent.shape
    degree_range = stored_coefficients.shape[1]
    rows = batch_size * parts
    peers = lax.axis_size("order")
    position = lax.axis_index("order")
    mine = lax.dynamic_slice_in_dim(order_table, position * slots, slots)
    table = picked_legendre(mine, degree_table, degree_range, latitude_count)
    table = table.reshape(peers, slots, slots, latitude_count)
    cot = cotangent.reshape(slots, latitude_count, rows, width)
    stored = stored_coefficients.reshape(slots, degree_range, rows, width)
    degrees = jnp.arange(degree_range).astype(jnp.int32)
    pick = (degree_table[:, None, None] == degrees[None, None, :]) & (
        degrees[None, None, :] >= mine[None, :, None]
    )
    pick = pick.astype(jnp.bfloat16).reshape(peers, slots, slots, degree_range)

    chunks = min(CHUNKS, slots)
    edges = [slots * i // chunks for i in range(chunks + 1)]
    spans = list(zip(edges[:-1], edges[1:]))

    def exchange(value):
        return lax.all_to_all(value, "order", split_axis=0, concat_axis=0, tiled=True)

    def project(matrix, source, lo, hi):
        return jnp.einsum(
            "tksj,sjrc->tkrsc", matrix[:, lo:hi], source, preferred_element_type=jnp.float32
        ).astype(jnp.bfloat16)

    saved, adjoint, gathered = [], [], []
    for lo, hi in spans:
        adjoint.append(exchange(project(table, cot, lo, hi)))
        gathered.append(lax.all_gather(adjoint[-1], "chan", axis=4, tiled=True))
    for lo, hi in spans:
        saved.append(exchange(project(pick, stored, lo, hi)))
    returned = []
    for i, (lo, hi) in enumerate(spans):
        coefficient = jnp.einsum(
            "nkrsd,kcd->nkrsc", gathered[i], weights[lo:hi], preferred_element_type=jnp.float32
        ).astype(jnp.bfloat16)
        returned.append(exchange(coefficient))
    mixing = []
    for i in range(chunks):
        mixing.append(
            jnp.einsum(
                "nkrsc,nkrsd->kcd", saved[i], gathered[i], preferred_element_type=jnp.float32
            ).astype(jnp.bfloat16)
        )
    mixing_gradient = jnp.concatenate(mixing, axis=0)
    back = jnp.concatenate(returned, axis=1)
    summed = jnp.einsum("tksj,tkrsc->sjrc", table, back, preferred_element_type=jnp.float32)
    quad = quadrature(latitude_count)
    input_gradient = (summed * quad[None, :, None, None]).astype(jnp.bfloat16)
    return input_gradient.reshape(cotangent.shape), mixing_gradient


def solution(mesh):
    return jax.shard_map(
        per_device,
        mesh=mesh,
        in_specs=(
            P("order", None, None, None, "chan"),
            P("order", None, None, None, "chan"),
            P("order", "chan", None),
            P(),
            P(),
        ),
        out_specs=(P("order", None, None, None, "chan"), P("order", "chan", None)),
        check_vma=False,
    )
```

time: 1300 us -> 659 us (0.51)
  local copies, waits for them, and re-layouts: 297 us -> 51.4 us
  other arithmetic: 229 us -> 27.1 us
  loops' own time: 164 us -> 0 us
  waiting for transfers between devices: 315 us -> 253 us
  matrix products: 76.9 us -> 93.1 us
    dynamic_update_slice x240 -> x0, other arithmetic: 169 us -> none  [legendre_rows(): lax.scan(advance, (zeros, zeros), jnp.arange(degree_range))]
    all_gather x1 -> x2, waiting for transfers between devices: 166 us -> 0.04 us  [per_device(): gathered.append(lax.all_gather(adjoint[-1], 'chan', axis=4, tiled=True))]
    another operation x1 -> x0, loops' own time: 164 us -> none  [legendre_rows(): lax.scan(advance, (zeros, zeros), jnp.arange(degree_range))]
    dynamic_slice x240 -> x0, local copies, waits for them, and re-layouts: 140 us -> none  [legendre_rows(): lax.scan(advance, (zeros, zeros), jnp.arange(degree_range))]
    all_to_all x2 -> x4, waiting for transfers between devices: 149 us -> 252 us  [exchange(): lax.all_to_all(value, 'order', split_axis=0, concat_axis=0, tiled=True)]
    reshape x5 -> x0, local copies, waits for them, and re-layouts: 75.3 us -> none  [the longest x1 17.9 us: per_device(): returned.reshape(slots, peers * slots, batch_size * 2 * slot_width)]
    gather x3 -> x0, local copies, waits for them, and re-layouts: 63.5 us -> none  [the longest x2 56.7 us: pack_rows(): picked = jnp.take(source, clipped, axis=1) * valid_bf[:, :, None, None]]
    mul x4 -> x3, other arithmetic: 38.3 us -> 0.72 us  [the longest x1 0.7 us: picked_legendre(): start = parity * jnp.exp(log_start + order_real * jnp.log(sine))]
  transfers between devices with their start and end apart: 3 -> 6, of which waited for: 2 -> 4; matrix products, arithmetic and copies ran while one was open for 6% -> 18% of each run, Pallas kernels for 0% -> 0%
where the time goes in v1:
time: 659 us; the launch traced here: 651 us
  waiting for transfers between devices  253 us (38%)
  blocking collectives  186 us (28%)
  matrix products  93.1 us (14%)
  local copies, waits for them, and re-layouts  51.4 us (8%)
  other arithmetic  27.1 us (4%)
  starting transfers between devices  19 us (3%)
  between operations  14.5 us (2%)
  Pallas kernels  7.52 us (1%)
    all_to_all x4, waiting for transfers between devices, exchange(): lax.all_to_all(value, 'order', split_axis=0, concat_axis=0, tiled=True)  252 us
    all_to_all x2, blocking collectives, exchange(): lax.all_to_all(value, 'order', split_axis=0, concat_axis=0, tiled=True)  186 us
    dot_general x2, matrix products, per_device(): jnp.einsum('nkrsc,nkrsd->kcd', saved[i], gathered[i], preferred_element_t...  30.6 us
    dot_general x4, matrix products, project(): jnp.einsum('tksj,sjrc->tkrsc', matrix[:, lo:hi], source, preferred_elemen...  23.9 us
    dot_general x2, matrix products, per_device(): jnp.einsum('nkrsd,kcd->nkrsc', gathered[i], weights[lo:hi], preferred_ele...  22.3 us
    all_to_all x4, starting transfers between devices, exchange(): lax.all_to_all(value, 'order', split_axis=0, concat_axis=0, tiled=True)  18.8 us
    dot_general x1, matrix products, per_device(): jnp.einsum('tksj,tkrsc->sjrc', table, back, preferred_element_type=jnp.fl...  16.3 us
    convert_element_type x2, local copies, waits for them, and re-layouts, per_device(): coefficient = jnp.einsum('nkrsd,kcd->nkrsc', gathered[i], weights[lo:hi],...  16.3 us
  transfers between devices with their start and end apart: 6, of which 4 were waited for; matrix products, arithmetic and copies ran while one was open for 18% of the time, Pallas kernels for 0%

profile of v1, /device:TPU:0, one launch (start us, length us, event | category | flops | bytes accessed | tf_op | source)
XLA Modules:
  0.0 650.9 jit_solution(14667385106930990605)
XLA Ops:
  7.2 0.0 all-gather.3.cloned.1.call-start
  7.4 0.8 select_reduce_fusion
  8.2 0.6 broadcast_minimum_fusion.where_ref
  8.8 0.8 fusion.52
  9.5 0.2 select_reduce_fusion.1
  9.7 0.7 exponential_multiply_fusion.start_ref
  10.4 9.1 %divide_sqrt_fusion = (f32[240,31,128]{2,1,0:T(8,128)}, f32[240,31,128]{2,1,0:T(8,128)}) fusion(f32[240]{0:T(256)S(1)} %get-tuple-element.15, f32[240]{0:T(256)S(1)} %get-tuple-element.17, f32[31]{0:T(128)S(1)} %get-tuple-element.11, f32[240]{0:T(256)S(1)} %get-tuple-element.16, f32[240]{0:T(256)S(1)} %get-tuple-element.14), kind=kLoop, calls=%fused_computation.37 | loop fusion | flops 5713920 | bytes 7622524 | tf_op jit(solution)/shard_map/sqrt | solution.py:68
  19.5 0.7 broadcast_in_dim.14.order_ref
  20.2 0.6 broadcast_in_dim.15.cosine_ref
  20.8 7.5 %legendre.1 = bf16[248,31,240]{2,1,0:T(8,128)(2,1)} custom-call(s32[240]{0:T(256)} %broadcast_minimum_fusion.where_ref, f32[240,31,128]{2,1,0:T(8,128)} %get-tuple-element.13.upper_ref, f32[240,31,128]{2,1,0:T(8,128)} %get-tuple-element.12.lower_ref, s32[31,128]{1,0:T(8,128)} %broadcast_in_dim.14.order_ref, f32[31,240]{1,0:T(8,128)} %broadcast_in_dim.15.cosine_ref, ...), custom_call_target="tpu_custom_call" | custom-call | flops 10713600 | bytes 25165824 | tf_op jit(solution)/shard_map/legendre/pallas_call | solution.py:80
  28.3 1.7 slice.24
  30.0 5.9 convert_bitcast_fusion.4
  35.9 3.0 copy.31
  38.9 92.3 %all_to_all.30 = bf16[8,15,2,31,256]{4,2,3,1,0:T(2,128)(2,1)S(1)} all-to-all(bf16[8,15,2,31,256]{4,2,3,1,0:T(2,128)(2,1)S(1)} %copy.31), channel_id=1, replica_groups=mesh['order'=8,'chan'=4] {'order'}, dimensions={0} | all-to-all | bytes 7618560 | tf_op jit(solution)/shard_map/all_to_all | solution.py:128
  131.2 3.0 copy.32
  134.2 0.0 all-gather.3.cloned.1.call-update
  134.2 0.2 all-gather.5.cloned.1.call-start
  134.5 1.8 slice.25
  136.3 6.3 convert_bitcast_fusion.3
  142.6 0.4 copy.36
  143.1 93.4 %all_to_all.31 = bf16[8,16,2,31,256]{4,1,2,3,0:T(8,128)(2,1)S(1)} all-to-all(bf16[8,16,2,31,256]{4,1,2,3,0:T(8,128)(2,1)S(1)} %copy.36), channel_id=1, replica_groups=mesh['order'=8,'chan'=4] {'order'}, dimensions={0} | all-to-all | bytes 8126464 | tf_op jit(solution)/shard_map/all_to_all | solution.py:128
  236.4 0.0 copy-start
  236.4 4.4 copy.37
  240.8 0.0 all-gather.5.cloned.1.call-update
  240.8 0.0 copy-done
  240.8 0.1 eq.38
  240.9 0.1 iota_compare_fusion.2
  241.0 0.1 iota_compare_fusion
  241.1 1.2 broadcast_and_fusion
  242.3 4.6 convert_bitcast_fusion.2
  246.9 5.4 copy.43
  252.3 5.0 all-to-all-start.4
  257.3 7.1 %convert_bitcast_fusion.1 = bf16[8,16,2,31,256]{4,1,3,2,0:T(8,128)(2,1)} fusion(bf16[31,240,2,256]{3,2,1,0:T(2,128)(2,1)} %bitcast.89, pred[8,31,31,240]{3,1,0,2:T(8,128)(4,1)S(1)} %broadcast_and_fusion), kind=kOutput, calls=%fused_computation.27 | convolution fusion | flops 977207296 | bytes 12697600 | tf_op jit(solution)/shard_map/tksj,sjrc->tkrsc/dot_general | solution.py:131
  264.4 76.4 %all-to-all-done.4 = bf16[8,15,2,31,256]{4,2,3,1,0:T(2,128)(2,1)} async-done(((bf16[8,15,2,31,256]{4,2,3,1,0:T(2,128)(2,1)}), bf16[8,15,2,31,256]{4,2,3,1,0:T(2,128)(2,1)}, u32[]{:S(2)}, u32[]{:S(2)}) %all-to-all-start.4) | async-done | bytes 3809312 | tf_op jit(solution)/shard_map/all_to_all | solution.py:128
  340.8 4.5 all-to-all-start.5
  345.3 0.0 all-gather.3.cloned.1.call-done
  345.3 10.4 %convert_bitcast_fusion.5 = bf16[8,15,2,31,256]{4,3,2,0,1:T(8,128)(2,1)S(1)} fusion(bf16[8,15,2,31,1024]{4,3,2,0,1:T(8,128)(2,1)} %all-gather.3.cloned.1.call-done, bf16[31,256,1024]{2,1,0:T(8,128)(2,1)} %param.7), kind=kOutput, calls=%fused_computation.36 | convolution fusion | flops 3902607360 | bytes 27402240 | tf_op jit(solution)/shard_map/nkrsd,kcd->nkrsc/dot_general | solution.py:143
  355.7 9.6 %copy.33 = bf16[8,15,2,31,256]{4,2,3,1,0:T(2,128)(2,1)} copy(bf16[8,15,2,31,256]{4,3,2,0,1:T(8,128)(2,1)S(1)} %convert_bitcast_fusion.5) | data formatting | bytes 7618560 | tf_op jit(solution)/shard_map/convert_element_type | solution.py:145
  365.3 69.7 %all-to-all-done.5 = bf16[8,16,2,31,256]{4,1,3,2,0:T(8,128)(2,1)} async-done(((bf16[8,16,2,31,256]{4,1,3,2,0:T(8,128)(2,1)}), bf16[8,16,2,31,256]{4,1,3,2,0:T(8,128)(2,1)}, u32[]{:S(2)}, u32[]{:S(2)}) %all-to-all-start.5) | async-done | bytes 4063264 | tf_op jit(solution)/shard_map/all_to_all | solution.py:128
  435.0 4.7 all-to-all-start.1
  439.8 0.0 all-gather.5.cloned.1.call-done
  439.9 11.9 %convert_bitcast_fusion = bf16[8,16,2,31,256]{4,3,2,0,1:T(8,128)(2,1)} fusion(bf16[8,16,2,31,1024]{4,3,2,0,1:T(8,128)(2,1)} %all-gather.5.cloned.1.call-done, bf16[31,256,1024]{2,1,0:T(8,128)(2,1)} %param.7), kind=kOutput, calls=%fused_computation.25 | convolution fusion | flops 4162781184 | bytes 29229056 | tf_op jit(solution)/shard_map/nkrsd,kcd->nkrsc/dot_general | solution.py:143
  451.8 6.7 %copy.38 = bf16[8,16,2,31,256]{4,1,2,3,0:T(8,128)(2,1)} copy(bf16[8,16,2,31,256]{4,3,2,0,1:T(8,128)(2,1)} %convert_bitcast_fusion) | data formatting | bytes 8126464 | tf_op jit(solution)/shard_map/convert_element_type | solution.py:145
  458.5 65.6 %all-to-all-done.1 = bf16[8,15,2,31,256]{4,2,3,1,0:T(2,128)(2,1)} async-done(((bf16[8,15,2,31,256]{4,2,3,1,0:T(2,128)(2,1)}), bf16[8,15,2,31,256]{4,2,3,1,0:T(2,128)(2,1)}, u32[]{:S(2)}, u32[]{:S(2)}) %all-to-all-start.1) | async-done | bytes 3809312 | tf_op jit(solution)/shard_map/all_to_all | solution.py:128
  524.1 4.5 all-to-all-start.3
  528.6 14.1 %bitcast_convert_fusion.1 = bf16[15,256,1024]{2,1,0:T(8,128)(2,1)} fusion(bf16[8,15,2,31,1024]{4,3,2,0,1:T(8,128)(2,1)} %all-gather.3.cloned.1.call-done, bf16[8,15,2,31,256]{4,2,3,1,0:T(2,128)(2,1)} %all-to-all-done.4), kind=kOutput, calls=%fused_computation.2 | convolution fusion | flops 3904634880 | bytes 26910720 | tf_op jit(solution)/shard_map/nkrsc,nkrsd->kcd/dot_general | solution.py:150
  542.7 16.5 %bitcast_convert_fusion = bf16[16,256,1024]{2,1,0:T(8,128)(2,1)} fusion(bf16[8,16,2,31,1024]{4,3,2,0,1:T(8,128)(2,1)} %all-gather.5.cloned.1.call-done, bf16[8,16,2,31,256]{4,1,3,2,0:T(8,128)(2,1)} %all-to-all-done.5), kind=kOutput, calls=%fused_computation | convolution fusion | flops 4164943872 | bytes 28704768 | tf_op jit(solution)/shard_map/nkrsc,nkrsd->kcd/dot_general | solution.py:150
  559.2 13.5 %pad_maximum_fusion = bf16[31,256,1024]{2,1,0:T(8,128)(2,1)} fusion(bf16[16,256,1024]{2,1,0:T(8,128)(2,1)} %bitcast_convert_fusion, bf16[15,256,1024]{2,1,0:T(8,128)(2,1)} %bitcast_convert_fusion.1), kind=kLoop, calls=%fused_computation.1 | loop fusion | flops 8126464 | bytes 32505856 | tf_op jit(solution)/shard_map/concatenate | solution.py:154
  572.7 4.8 copy.39
  577.6 40.8 %all-to-all-done.3 = bf16[8,16,2,31,256]{4,1,2,3,0:T(8,128)(2,1)} async-done(((bf16[8,16,2,31,256]{4,1,2,3,0:T(8,128)(2,1)}), bf16[8,16,2,31,256]{4,1,2,3,0:T(8,128)(2,1)}, u32[]{:S(2)}, u32[]{:S(2)}) %all-to-all-start.3) | async-done | bytes 4063264 | tf_op jit(solution)/shard_map/all_to_all | solution.py:128
  618.4 16.3 %fusion.19 = bf16[31,240,1,2,256]{4,1,3,0,2:T(8,128)(2,1)S(1)} fusion(f32[240]{0:T(256)S(1)} %fusion.48, bf16[8,15,2,31,256]{4,1,0,2,3:T(8,128)(2,1)} %copy.39, bf16[8,31,31,240,1]{3,2,1,0,4:T(8,128)(2,1)} %bitcast.87, bf16[8,16,2,31,256]{4,1,2,3,0:T(8,128)(2,1)} %all-to-all-done.3), kind=kOutput, calls=%fused_computation.23 | convolution fusion | flops 1912766464 | bytes 19182272 | tf_op jit(solution)/shard_map/tksj,tkrsc->sjrc/dot_general | solution.py:156
  634.7 9.2 %copy.48 = bf16[31,240,1,2,256]{4,3,2,1,0:T(2,128)(2,1)} copy(bf16[31,240,1,2,256]{4,1,3,0,2:T(8,128)(2,1)S(1)} %fusion.19) | data formatting | bytes 15237120
  (9 shorter events, 0.2 us)
Async XLA Ops:
  7.2 338.2 %all-gather.3.cloned.1.call-start = ((), (), s32[]{:S(2)}) async-start(), calls=%async_computation.6 | async-start | bytes 19660800 | tf_op jit(solution)/shard_map/all_gather | solution.py:138
  134.2 305.6 %all-gather.5.cloned.1.call-start = ((), (), s32[]{:S(2)}) async-start(), calls=%async_computation.7 | async-start | bytes 20971520 | tf_op jit(solution)/shard_map/all_gather | solution.py:138
  236.4 4.4 copy-start
  252.3 88.5 %all-to-all-start.4 = ((bf16[8,15,2,31,256]{4,2,3,1,0:T(2,128)(2,1)}), bf16[8,15,2,31,256]{4,2,3,1,0:T(2,128)(2,1)}, u32[]{:S(2)}, u32[]{:S(2)}) async-start(bf16[8,15,2,31,256]{4,2,3,1,0:T(2,128)(2,1)} %copy.43), calls=%async_computation.4 | async-start | bytes 7618560 | tf_op jit(solution)/shard_map/all_to_all | solution.py:128
  340.8 94.3 %all-to-all-start.5 = ((bf16[8,16,2,31,256]{4,1,3,2,0:T(8,128)(2,1)}), bf16[8,16,2,31,256]{4,1,3,2,0:T(8,128)(2,1)}, u32[]{:S(2)}, u32[]{:S(2)}) async-start(bf16[8,16,2,31,256]{4,1,3,2,0:T(8,128)(2,1)} %convert_bitcast_fusion.1), calls=%async_computation.5 | async-start | bytes 8126464 | tf_op jit(solution)/shard_map/all_to_all | solution.py:128
  435.0 89.0 %all-to-all-start.1 = ((bf16[8,15,2,31,256]{4,2,3,1,0:T(2,128)(2,1)}), bf16[8,15,2,31,256]{4,2,3,1,0:T(2,128)(2,1)}, u32[]{:S(2)}, u32[]{:S(2)}) async-start(bf16[8,15,2,31,256]{4,2,3,1,0:T(2,128)(2,1)} %copy.33), calls=%async_computation.1 | async-start | bytes 7618560 | tf_op jit(solution)/shard_map/all_to_all | solution.py:128
  524.1 94.3 %all-to-all-start.3 = ((bf16[8,16,2,31,256]{4,1,2,3,0:T(8,128)(2,1)}), bf16[8,16,2,31,256]{4,1,2,3,0:T(8,128)(2,1)}, u32[]{:S(2)}, u32[]{:S(2)}) async-start(bf16[8,16,2,31,256]{4,1,2,3,0:T(8,128)(2,1)} %copy.38), calls=%async_computation.3 | async-start | bytes 8126464 | tf_op jit(solution)/shard_map/all_to_all | solution.py:128
Sparse Core Ops, SparseCore 0:
  134.3 100.7 all-gather.2
  240.9 106.7 all-gather.4

commit v2 on v1

--- a/solution.py
+++ b/solution.py
@@ -7,7 +7,7 @@
 from jax.experimental.pallas import tpu as pltpu
 from jax.sharding import PartitionSpec as P
 
-CHUNKS = 2
+SPREADS = 3.5
 LANES = 128
 
 
@@ -103,60 +103,117 @@
     return jnp.pi / latitude_count * jnp.sin(angles)
 
 
-def per_device(cotangent, stored_coefficients, weights, order_table, degree_table):
+def dense_exchange(peers, slots):
+    def exchange(value):
+        moved = lax.all_to_all(
+            value.reshape(peers, slots, slots, value.shape[-1]),
+            "order",
+            split_axis=0,
+            concat_axis=0,
+            tiled=True,
+        )
+        return moved
+
+    return exchange, exchange
+
+
+def packed_exchange(peers, slots, capacity, leave, arrive):
+    place = jnp.arange(capacity).astype(jnp.int32)[None, :, None, None]
+    leave_matrix = (leave[:, None] == place).astype(jnp.bfloat16)
+    arrive_matrix = (arrive[:, None] == place).astype(jnp.bfloat16)
+
+    def route(value, packer, unpacker):
+        packed = jnp.einsum(
+            "tpks,tksc->tpc", packer, value, preferred_element_type=jnp.float32
+        ).astype(jnp.bfloat16)
+        moved = lax.all_to_all(packed, "order", split_axis=0, concat_axis=0, tiled=True)
+        return jnp.einsum(
+            "tpks,tpc->tksc", unpacker, moved, preferred_element_type=jnp.float32
+        ).astype(jnp.bfloat16)
+
+    return (
+        lambda value: route(value, leave_matrix, arrive_matrix),
+        lambda value: route(value, arrive_matrix, leave_matrix),
+    )
+
+
+def layer(send, back, cotangent, stored_coefficients, weights, table, pick):
     slots, latitude_count, batch_size, parts, width = cotangent.shape
     degree_range = stored_coefficients.shape[1]
     rows = batch_size * parts
+    cot = cotangent.reshape(slots, latitude_count, rows, width)
+    stored = stored_coefficients.reshape(slots, degree_range, rows, width)
+
+    def project(matrix, source):
+        return jnp.einsum(
+            "tksj,sjc->tksc", matrix, source, preferred_element_type=jnp.float32
+        ).astype(jnp.bfloat16)
+
+    gathered, saved, mixing, outputs = [], [], [], []
+    for r in range(rows):
+        adjoint = send(project(table, cot[:, :, r]))
+        gathered.append(lax.all_gather(adjoint, "chan", axis=3, tiled=True))
+    for r in range(rows):
+        saved.append(send(project(pick, stored[:, :, r])))
+    quad = quadrature(latitude_count)
+    for r in range(rows):
+        coefficient = jnp.einsum(
+            "nksd,kcd->nksc", gathered[r], weights, preferred_element_type=jnp.float32
+        ).astype(jnp.bfloat16)
+        summed = jnp.einsum(
+            "tksj,tksc->sjc", table, back(coefficient), preferred_element_type=jnp.float32
+        )
+        outputs.append((summed * quad[None, :, None]).astype(jnp.bfloat16))
+    for r in range(rows):
+        mixing.append(
+            jnp.einsum("nksc,nksd->kcd", saved[r], gathered[r], preferred_element_type=jnp.float32)
+        )
+    mixing_gradient = sum(mixing[1:], mixing[0]).astype(jnp.bfloat16)
+    return jnp.stack(outputs, axis=2).reshape(cotangent.shape), mixing_gradient
+
+
+def per_device(cotangent, stored_coefficients, weights, order_table, degree_table):
+    slots, latitude_count = cotangent.shape[:2]
+    degree_range = stored_coefficients.shape[1]
     peers = lax.axis_size("order")
     position = lax.axis_index("order")
     mine = lax.dynamic_slice_in_dim(order_table, position * slots, slots)
+    owned = lax.dynamic_slice_in_dim(degree_table, position * slots, slots)
     table = picked_legendre(mine, degree_table, degree_range, latitude_count)
     table = table.reshape(peers, slots, slots, latitude_count)
-    cot = cotangent.reshape(slots, latitude_count, rows, width)
-    stored = stored_coefficients.reshape(slots, degree_range, rows, width)
     degrees = jnp.arange(degree_range).astype(jnp.int32)
     pick = (degree_table[:, None, None] == degrees[None, None, :]) & (
         degrees[None, None, :] >= mine[None, :, None]
     )
     pick = pick.astype(jnp.bfloat16).reshape(peers, slots, slots, degree_range)
-
-    chunks = min(CHUNKS, slots)
-    edges = [slots * i // chunks for i in range(chunks + 1)]
-    spans = list(zip(edges[:-1], edges[1:]))
-
-    def exchange(value):
-        return lax.all_to_all(value, "order", split_axis=0, concat_axis=0, tiled=True)
-
-    def project(matrix, source, lo, hi):
-        return jnp.einsum(
-            "tksj,sjrc->tkrsc", matrix[:, lo:hi], source, preferred_element_type=jnp.float32
-        ).astype(jnp.bfloat16)
-
-    saved, adjoint, gathered = [], [], []
-    for lo, hi in spans:
-        adjoint.append(exchange(project(table, cot, lo, hi)))
-        gathered.append(lax.all_gather(adjoint[-1], "chan", axis=4, tiled=True))
-    for lo, hi in spans:
-        saved.append(exchange(project(pick, stored, lo, hi)))
-    returned = []
-    for i, (lo, hi) in enumerate(spans):
-        coefficient = jnp.einsum(
-            "nkrsd,kcd->nkrsc", gathered[i], weights[lo:hi], preferred_element_type=jnp.float32
-        ).astype(jnp.bfloat16)
-        returned.append(exchange(coefficient))
-    mixing = []
-    for i in range(chunks):
-        mixing.append(
-            jnp.einsum(
-                "nkrsc,nkrsd->kcd", saved[i], gathered[i], preferred_element_type=jnp.float32
-            ).astype(jnp.bfloat16)
-        )
-    mixing_gradient = jnp.concatenate(mixing, axis=0)
-    back = jnp.concatenate(returned, axis=1)
-    summed = jnp.einsum("tksj,tkrsc->sjrc", table, back, preferred_element_type=jnp.float32)
-    quad = quadrature(latitude_count)
-    input_gradient = (summed * quad[None, :, None, None]).astype(jnp.bfloat16)
-    return input_gradient.reshape(cotangent.shape), mixing_gradient
+    operands = (cotangent, stored_coefficients, weights, table, pick)
+
+    full = slots * slots
+    live = degree_range * (degree_range + 1) / 2 / (peers * slots) ** 2
+    spread = (full * (2 * slots + 1) / 12) ** 0.5
+    capacity = -(-int(live * full + SPREADS * spread) // 16) * 16
+    dense = functools.partial(layer, *dense_exchange(peers, slots))
+    if capacity > 0.85 * full:
+        return dense(*operands)
+
+    def places(orders, degree_rows):
+        valid = (degree_rows >= orders) & (degree_rows < degree_range)
+        flags = valid.reshape(-1, full).astype(jnp.bfloat16)
+        index = jnp.arange(full)
+        before = (index[:, None] < index[None, :]).astype(jnp.bfloat16)
+        rank = jnp.dot(flags, before, preferred_element_type=jnp.float32).astype(jnp.int32)
+        return jnp.where(valid, rank.reshape(valid.shape), -1)
+
+    leave = places(mine[None, None, :], degree_table.reshape(peers, slots)[:, :, None])
+    arrive = places(order_table.reshape(peers, slots)[:, None, :], owned[None, :, None])
+    order_rows = order_table.reshape(peers, 1, slots, 1)
+    degree_rows = degree_table.reshape(1, peers, 1, slots)
+    counts = jnp.sum(
+        ((degree_rows >= order_rows) & (degree_rows < degree_range)).astype(jnp.int32), axis=(2, 3)
+    )
+    fits = jnp.max(counts) <= capacity
+    packed = functools.partial(layer, *packed_exchange(peers, slots, capacity, leave, arrive))
+    return lax.cond(fits, packed, dense, *operands)
 
 
 def solution(mesh):

time: 659 us -> 587 us (0.89)
  waiting for transfers between devices: 253 us -> 125 us
  matrix products: 93.1 us -> 200 us
  blocking collectives: 186 us -> 140 us
  local copies, waits for them, and re-layouts: 51.4 us -> 34.1 us
  loops' own time: 0 us -> 8.82 us
  other arithmetic: 27.1 us -> 34.1 us
    all_to_all x4, waiting for transfers between devices: 252 us -> 125 us  [route(): lax.all_to_all(packed, 'order', split_axis=0, concat_axis=0, tiled=True)]
    dot_general x9 -> x17, matrix products: 93.1 us -> 200 us  [the longest x6 71.7 us: route(): jnp.einsum('tpks,tksc->tpc', packer, value, preferred_element_type=jnp.fl...]
    all_to_all x2, blocking collectives: 186 us -> 140 us  [route(): lax.all_to_all(packed, 'order', split_axis=0, concat_axis=0, tiled=True)]
    another operation x0 -> x7, local copies, waits for them, and re-layouts: none -> 26.6 us
    convert_element_type x5 -> x0, local copies, waits for them, and re-layouts: 25.1 us -> none  [the longest x2 16.3 us: per_device(): coefficient = jnp.einsum('nkrsd,kcd->nkrsc', gathered[i], weights[lo:hi],...]
    convert_element_type x0 -> x3, other arithmetic: none -> 15 us  [the longest x1 6.11 us: packed_exchange(): arrive_matrix = (arrive[:, None] == place).astype(jnp.bfloat16)]
    concatenate x1 -> x0, other arithmetic: 13.5 us -> none  [per_device(): mixing_gradient = jnp.concatenate(mixing, axis=0)]
    all_to_all x3 -> x0, local copies, waits for them, and re-layouts: 12.2 us -> none  [exchange(): lax.all_to_all(value, 'order', split_axis=0, concat_axis=0, tiled=True)]
  transfers between devices with their start and end apart: 6 -> 6, of which waited for: 4 -> 4; matrix products, arithmetic and copies ran while one was open for 18% -> 30% of each run, Pallas kernels for 0% -> 0%
where the time goes in v2:
time: 587 us; the launch traced here: 581 us
  matrix products  200 us (34%)
  blocking collectives  140 us (24%)
  waiting for transfers between devices  125 us (21%)
  other arithmetic  34.1 us (6%)
  local copies, waits for them, and re-layouts  34.1 us (6%)
  starting transfers between devices  16.4 us (3%)
  between operations  15 us (3%)
  loops' own time  8.82 us (2%)
  Pallas kernels  7.51 us (1%)
    all_to_all x2, blocking collectives, route(): lax.all_to_all(packed, 'order', split_axis=0, concat_axis=0, tiled=True)  140 us
    all_to_all x4, waiting for transfers between devices, route(): lax.all_to_all(packed, 'order', split_axis=0, concat_axis=0, tiled=True)  125 us
    dot_general x6, matrix products, route(): jnp.einsum('tpks,tksc->tpc', packer, value, preferred_element_type=jnp.fl...  71.7 us
    dot_general x2, matrix products, layer(): jnp.einsum('nksc,nksd->kcd', saved[r], gathered[r], preferred_element_typ...  45.6 us
    dot_general x3, matrix products, route(): jnp.einsum('tpks,tpc->tksc', unpacker, moved, preferred_element_type=jnp....  30.9 us
    dot_general x2, matrix products, layer(): jnp.einsum('nksd,kcd->nksc', gathered[r], weights, preferred_element_type...  27.3 us
    another operation x7, local copies, waits for them, and re-layouts  26.6 us
    dot_general x2, matrix products, layer(): jnp.einsum('tksj,tksc->sjc', table, back(coefficient), preferred_element_...  23.9 us
  transfers between devices with their start and end apart: 6, of which 4 were waited for; matrix products, arithmetic and copies ran while one was open for 30% of the time, Pallas kernels for 0%

profile of v2, /device:TPU:0, one launch (start us, length us, event | category | flops | bytes accessed | tf_op | source)
XLA Modules:
  0.0 581.0 jit_solution(402957501516819246)
XLA Ops:
  7.2 0.8 select_reduce_fusion
  8.0 0.6 broadcast_minimum_fusion.where_ref
  8.7 0.8 fusion.184
  9.4 0.2 select_reduce_fusion.1
  9.6 0.8 broadcast_compare_fusion.1
  10.4 0.8 ge.91
  11.2 0.8 ge.93
  11.9 0.5 convert_reduce_fusion
  12.5 0.6 reduce_max.9
  13.9 0.1 and.79
  14.1 0.1 ge.111
  14.2 0.1 ge.104
  14.3 0.7 broadcast_in_dim.22.order_ref
  15.0 0.7 exponential_multiply_fusion.start_ref
  15.7 0.6 broadcast_in_dim.23.cosine_ref
  16.3 0.1 and.72
  16.4 0.1 and.74
  16.5 0.1 iota_compare_fusion.9
  16.7 0.1 ge.113
  16.8 0.3 fusion.167
  17.1 0.2 reshape.216
  17.6 0.1 ge.102
  17.7 0.3 fusion.166
  18.0 0.2 reshape.215
  18.2 0.1 and_select_fusion.1
  18.3 0.1 copy.82
  18.4 3.0 and_convert_fusion
  21.4 9.1 %divide_sqrt_fusion = (f32[240,31,128]{2,1,0:T(8,128)}, f32[240,31,128]{2,1,0:T(8,128)}) fusion(f32[240]{0:T(256)S(1)} %get-tuple-element.114, f32[240]{0:T(256)S(1)} %get-tuple-element.116, f32[31]{0:T(128)S(1)} %get-tuple-element.110, f32[240]{0:T(256)S(1)} %get-tuple-element.115, f32[240]{0:T(256)S(1)} %get-tuple-element.113), kind=kLoop, calls=%fused_computation.138 | loop fusion | flops 5713920 | bytes 7622524 | tf_op jit(solution)/shard_map/sqrt | solution.py:68
  30.5 7.5 %legendre.1 = bf16[248,31,240]{2,1,0:T(8,128)(2,1)} custom-call(s32[240]{0:T(256)} %broadcast_minimum_fusion.where_ref, f32[240,31,128]{2,1,0:T(8,128)} %get-tuple-element.112.upper_ref, f32[240,31,128]{2,1,0:T(8,128)} %get-tuple-element.111.lower_ref, s32[31,128]{1,0:T(8,128)} %broadcast_in_dim.22.order_ref, f32[31,240]{1,0:T(8,128)} %broadcast_in_dim.23.cosine_ref, ...), custom_call_target="tpu_custom_call" | custom-call | flops 10713600 | bytes 25165824 | tf_op jit(solution)/shard_map/legendre/pallas_call | solution.py:80
  38.0 5.9 %fusion.162 = bf16[8,704,31,31]{1,2,0,3:T(8,128)(2,1)} fusion(s32[8,31,31]{1,0,2:T(8,128)S(1)} %copy.82), kind=kLoop, calls=%fused_computation.132 | loop fusion | flops 10824704 | bytes 10855456 | tf_op jit(solution)/shard_map/convert_element_type | solution.py:122
  44.0 6.1 %fusion.163 = bf16[8,704,31,31]{1,3,0,2:T(8,128)(2,1)} fusion(s32[8,31,31]{2,0,1:T(8,128)S(1)} %copy.83), kind=kLoop, calls=%fused_computation.133 | loop fusion | flops 10824704 | bytes 10855456 | tf_op jit(solution)/shard_map/convert_element_type | solution.py:123
  50.1 520.8 %conditional.3 = (bf16[31,256,1024]{2,1,0:T(8,128)(2,1)}, bf16[31,240,1,2,256]{4,3,2,1,0:T(2,128)(2,1)S(1)}) conditional(s32[]{:T(128)} %convert_element_type.278, (bf16[31,240,1,2,256]{4,3,2,1,0:T(2,128)(2,1)}, bf16[8,31,31,240]{3,2,1,0:T(8,128)(2,1)}, bf16[31,256,1024]{2,1,0:T(8,128)(2,1)}, bf16[31,240,1,2,256]{4,3,2,1,0:T(2,128)(2,1)}, ...), branch_computations={%region_4.5_spmd, %region_5.6_spmd} | conditional | flops 55100612608 | bytes 662673728
  58.7 7.4 %copy.183 = bf16[31,240,1,2,256]{4,1,0,3,2:T(8,128)(2,1)} copy(bf16[31,240,1,2,256]{4,3,2,1,0:T(2,128)(2,1)} %get-tuple-element.95) | data formatting | bytes 15237120 | tf_op jit(solution)/shard_map
  66.1 11.6 %fusion.98 = bf16[8,704,256]{2,1,0:T(8,128)(2,1)} fusion(bf16[8,704,31,31]{1,2,0,3:T(8,128)(2,1)} %get-tuple-element.39, bf16[8,31,31,240]{3,2,1,0:T(8,128)(2,1)} %get-tuple-element.96, bf16[31,240,2,256]{3,1,0,2:T(8,128)(2,1)} %bitcast.339), kind=kOutput, calls=%fused_computation.113 | convolution fusion | flops 3719235584 | bytes 22945792 | tf_op jit(solution)/shard_map/cond/branch_1_fun/tpks,tksc->tpc/dot_general | solution.py:126
  77.8 72.4 %all_to_all.50 = bf16[8,704,256]{2,1,0:T(8,128)(2,1)S(1)} all-to-all(bf16[8,704,256]{2,1,0:T(8,128)(2,1)} %fusion.98), channel_id=1, replica_groups=mesh['order'=8,'chan'=4] {'order'}, dimensions={0} | all-to-all | bytes 5767168 | tf_op jit(solution)/shard_map/cond/branch_1_fun/all_to_all | solution.py:129
  150.1 9.7 %convert_bitcast_fusion.7 = bf16[8,31,31,256]{3,2,1,0:T(8,128)(2,1)} fusion(bf16[8,704,31,31]{1,3,0,2:T(8,128)(2,1)} %get-tuple-element.40, bf16[8,704,256]{2,1,0:T(8,128)(2,1)S(1)} %all_to_all.50), kind=kOutput, calls=%fused_computation.99 | convolution fusion | flops 2773092352 | bytes 17644544 | tf_op jit(solution)/shard_map/cond/branch_1_fun/tpks,tpc->tksc/dot_general | solution.py:130
  159.9 11.0 %fusion.100 = bf16[8,704,256]{2,1,0:T(8,128)(2,1)S(1)} fusion(bf16[8,704,31,31]{1,2,0,3:T(8,128)(2,1)} %get-tuple-element.39, bf16[8,31,31,240]{3,2,1,0:T(8,128)(2,1)} %get-tuple-element.96, bf16[31,240,2,256]{3,1,0,2:T(8,128)(2,1)} %bitcast.340), kind=kOutput, calls=%fused_computation.115 | convolution fusion | flops 3719235584 | bytes 22945792 | tf_op jit(solution)/shard_map/cond/branch_1_fun/tpks,tksc->tpc/dot_general | solution.py:126
  170.9 67.6 %all_to_all.51 = bf16[8,704,256]{2,1,0:T(8,128)(2,1)} all-to-all(bf16[8,704,256]{2,1,0:T(8,128)(2,1)S(1)} %fusion.100), channel_id=1, replica_groups=mesh['order'=8,'chan'=4] {'order'}, dimensions={0} | all-to-all | bytes 5767168 | tf_op jit(solution)/shard_map/cond/branch_1_fun/all_to_all | solution.py:129
  238.5 10.6 %convert_bitcast_fusion.6 = bf16[8,31,31,256]{3,2,1,0:T(8,128)(2,1)} fusion(bf16[8,704,31,31]{1,3,0,2:T(8,128)(2,1)} %get-tuple-element.40, bf16[8,704,256]{2,1,0:T(8,128)(2,1)} %all_to_all.51), kind=kOutput, calls=%fused_computation.95 | convolution fusion | flops 2773092352 | bytes 17644544 | tf_op jit(solution)/shard_map/cond/branch_1_fun/tpks,tpc->tksc/dot_general | solution.py:130
  249.2 7.4 %copy.182 = bf16[31,240,1,2,256]{4,1,0,3,2:T(8,128)(2,1)} copy(bf16[31,240,1,2,256]{4,3,2,1,0:T(2,128)(2,1)} %get-tuple-element.100) | data formatting | bytes 15237120 | tf_op jit(solution)/shard_map
  256.6 11.7 %fusion.102 = bf16[8,704,256]{2,1,0:T(8,128)(2,1)} fusion(bf16[8,704,31,31]{1,2,0,3:T(8,128)(2,1)} %get-tuple-element.39, bf16[8,31,31,240]{3,1,0,2:T(8,128)(2,1)} %get-tuple-element.43, bf16[31,240,2,256]{3,1,0,2:T(8,128)(2,1)} %bitcast.343), kind=kOutput, calls=%fused_computation.117 | convolution fusion | flops 3719235584 | bytes 22945792 | tf_op jit(solution)/shard_map/cond/branch_1_fun/tpks,tksc->tpc/dot_general | solution.py:126
  268.3 3.6 all-to-all-start.10
  271.9 0.6 sine_multiply_fusion.1
  272.5 14.6 %fusion.103 = bf16[8,704,256]{2,1,0:T(8,128)(2,1)} fusion(bf16[8,704,31,31]{1,2,0,3:T(8,128)(2,1)} %get-tuple-element.39, bf16[8,31,31,240]{3,1,0,2:T(8,128)(2,1)} %get-tuple-element.43, bf16[31,240,2,256]{3,1,0,2:T(8,128)(2,1)} %bitcast.344), kind=kOutput, calls=%fused_computation.118 | convolution fusion | flops 3719235584 | bytes 22945792 | tf_op jit(solution)/shard_map/cond/branch_1_fun/tpks,tksc->tpc/dot_general | solution.py:126
  287.2 48.6 %all-to-all-done.10 = bf16[8,704,256]{2,1,0:T(8,128)(2,1)S(1)} async-done(((bf16[8,704,256]{2,1,0:T(8,128)(2,1)}), bf16[8,704,256]{2,1,0:T(8,128)(2,1)S(1)}, u32[]{:S(2)}, u32[]{:S(2)}) %all-to-all-start.10) | async-done | bytes 2883616 | tf_op jit(solution)/shard_map/cond/branch_1_fun/all_to_all | solution.py:129
  335.7 1.6 copy-done.4
  337.4 3.9 all-to-all-start.11
  341.3 10.6 %fusion.215 = bf16[8,31,31,256]{3,2,0,1:T(8,128)(2,1)} fusion(bf16[8,704,31,31]{1,3,0,2:T(8,128)(2,1)} %get-tuple-element.40, bf16[8,704,256]{2,1,0:T(8,128)(2,1)} %copy-done.4), kind=kOutput, calls=%fused_computation.72.clone.1 | convolution fusion | flops 2773092352 | bytes 17644544 | tf_op jit(solution)/shard_map/cond/branch_1_fun/tpks,tpc->tksc/dot_general | solution.py:130
  351.9 13.7 %fusion.40 = bf16[31,8,31,256]{3,2,1,0:T(8,128)(2,1)} fusion(bf16[31,256,1024]{2,1,0:T(8,128)(2,1)} %get-tuple-element.41, bf16[8,31,31,1024]{3,2,1,0:T(8,128)(2,1)} %all-gather.9.cloned.1.call-done), kind=kOutput, calls=%fused_computation.44 | convolution fusion | flops 4030726144 | bytes 35934208 | tf_op jit(solution)/shard_map/cond/branch_1_fun/nksd,kcd->nksc/dot_general | solution.py:160
  365.5 11.7 %fusion.99 = bf16[8,704,256]{2,1,0:T(8,128)(2,1)} fusion(bf16[8,704,31,31]{1,3,0,2:T(8,128)(2,1)} %get-tuple-element.40, bf16[31,8,31,256]{3,2,1,0:T(8,128)(2,1)} %fusion.40), kind=kOutput, calls=%fused_computation.114 | convolution fusion | flops 2772566016 | bytes 17644544 | tf_op jit(solution)/shard_map/cond/branch_1_fun/tpks,tksc->tpc/dot_general | solution.py:126
  377.2 13.7 %fusion.38 = bf16[31,8,31,256]{3,2,1,0:T(8,128)(2,1)} fusion(bf16[31,256,1024]{2,1,0:T(8,128)(2,1)} %get-tuple-element.41, bf16[8,31,31,1024]{3,2,1,0:T(8,128)(2,1)} %all-gather.11.cloned.1.call-done), kind=kOutput, calls=%fused_computation.42 | convolution fusion | flops 4030726144 | bytes 35934208 | tf_op jit(solution)/shard_map/cond/branch_1_fun/nksd,kcd->nksc/dot_general | solution.py:160
  390.9 15.6 %all-to-all-done.11 = bf16[8,704,256]{2,1,0:T(8,128)(2,1)S(1)} async-done(((bf16[8,704,256]{2,1,0:T(8,128)(2,1)}), bf16[8,704,256]{2,1,0:T(8,128)(2,1)S(1)}, u32[]{:S(2)}, u32[]{:S(2)}) %all-to-all-start.11) | async-done | bytes 2883616 | tf_op jit(solution)/shard_map/cond/branch_1_fun/all_to_all | solution.py:129
  406.5 4.7 all-to-all-start.7
  411.2 11.0 %fusion.101 = bf16[8,704,256]{2,1,0:T(8,128)(2,1)} fusion(bf16[8,704,31,31]{1,3,0,2:T(8,128)(2,1)} %get-tuple-element.40, bf16[31,8,31,256]{3,2,1,0:T(8,128)(2,1)} %fusion.38), kind=kOutput, calls=%fused_computation.116 | convolution fusion | flops 2772566016 | bytes 17644544 | tf_op jit(solution)/shard_map/cond/branch_1_fun/tpks,tksc->tpc/dot_general | solution.py:126
  422.2 21.4 %fusion.42 = f32[31,256,1024,1]{2,1,3,0:T(8,128)} fusion(bf16[8,31,31,1024]{3,2,1,0:T(8,128)(2,1)} %all-gather.11.cloned.1.call-done, bf16[8,704,31,31]{1,3,0,2:T(8,128)(2,1)} %get-tuple-element.40, bf16[8,704,256]{2,1,0:T(8,128)(2,1)S(1)} %all-to-all-done.11), kind=kOutput, calls=%fused_computation.46 | convolution fusion | flops 6803818496 | bytes 61959168 | tf_op jit(solution)/shard_map/cond/branch_1_fun/nksc,nksd->kcd/dot_general | solution.py:169
  443.5 32.2 %all-to-all-done.7 = bf16[8,704,256]{2,1,0:T(8,128)(2,1)} async-done(((bf16[8,704,256]{2,1,0:T(8,128)(2,1)}), bf16[8,704,256]{2,1,0:T(8,128)(2,1)}, u32[]{:S(2)}, u32[]{:S(2)}) %all-to-all-start.7) | async-done | bytes 2883616 | tf_op jit(solution)/shard_map/cond/branch_1_fun/all_to_all | solution.py:129
  475.8 4.1 all-to-all-start.9
  479.9 24.3 %fusion.37 = bf16[31,256,1024]{2,1,0:T(8,128)(2,1)} fusion(f32[31,256,1024,1]{2,1,3,0:T(8,128)} %fusion.42, bf16[8,31,31,1024]{3,2,1,0:T(8,128)(2,1)} %all-gather.9.cloned.1.call-done, bf16[8,31,31,256]{3,2,0,1:T(8,128)(2,1)} %fusion.215), kind=kOutput, calls=%fused_computation.41 | convolution fusion | flops 4046979072 | bytes 68440064 | tf_op jit(solution)/shard_map/cond/branch_1_fun/nksc,nksd->kcd/dot_general | solution.py:169
  504.2 12.4 %fusion.92 = bf16[31,240,1,256]{3,1,0,2:T(8,128)(2,1)} fusion(f32[240]{0:T(256)S(1)} %copy-done.5, bf16[8,31,31,240]{3,2,1,0:T(8,128)(2,1)} %get-tuple-element.96, bf16[8,704,31,31]{1,2,0,3:T(8,128)(2,1)} %get-tuple-element.39, bf16[8,704,256]{2,1,0:T(8,128)(2,1)} %all-to-all-done.7), kind=kOutput, calls=%fused_computation.103 | convolution fusion | flops 3721603072 | bytes 21208768 | tf_op jit(solution)/shard_map/cond/branch_1_fun/tksj,tksc->sjc/dot_general | solution.py:163
  516.6 28.5 %all-to-all-done.9 = bf16[8,704,256]{2,1,0:T(8,128)(2,1)S(1)} async-done(((bf16[8,704,256]{2,1,0:T(8,128)(2,1)}), bf16[8,704,256]{2,1,0:T(8,128)(2,1)S(1)}, u32[]{:S(2)}, u32[]{:S(2)}) %all-to-all-start.9) | async-done | bytes 2883616 | tf_op jit(solution)/shard_map/cond/branch_1_fun/all_to_all | solution.py:129
  545.1 11.5 %fusion.93 = bf16[31,240,1,256]{3,1,0,2:T(8,128)(2,1)} fusion(f32[240]{0:T(256)S(1)} %copy-done.5, bf16[8,31,31,240]{3,2,1,0:T(8,128)(2,1)} %get-tuple-element.96, bf16[8,704,31,31]{1,2,0,3:T(8,128)(2,1)} %get-tuple-element.39, bf16[8,704,256]{2,1,0:T(8,128)(2,1)S(1)} %all-to-all-done.9), kind=kOutput, calls=%fused_computation.104 | convolution fusion | flops 3721603072 | bytes 21208768 | tf_op jit(solution)/shard_map/cond/branch_1_fun/tksj,tksc->sjc/dot_general | solution.py:163
  556.6 3.9 maximum_bitcast_fusion.1
  560.6 10.1 %copy.110 = bf16[31,240,1,2,256]{4,3,2,1,0:T(2,128)(2,1)S(1)} copy(bf16[31,240,1,2,256]{4,1,0,3,2:T(8,128)(2,1)S(1)} %maximum_bitcast_fusion.1) | data formatting | bytes 15237120 | tf_op jit(solution)/shard_map/conditional.1
  570.9 3.1 copy-done.3
  (27 shorter events, 0.8 us)
Async XLA Ops:
  58.6 293.3 %all-gather.9.cloned.1.call-start = ((), (), s32[]{:S(2)}) async-start(), calls=%async_computation.14 | async-start | bytes 20316160 | tf_op jit(solution)/shard_map/cond/branch_1_fun/all_gather | solution.py:155
  159.8 217.4 %all-gather.11.cloned.1.call-start = ((), (), s32[]{:S(2)}) async-start(), calls=%async_computation.15 | async-start | bytes 20316160 | tf_op jit(solution)/shard_map/cond/branch_1_fun/all_gather | solution.py:155
  268.3 67.5 %all-to-all-start.10 = ((bf16[8,704,256]{2,1,0:T(8,128)(2,1)}), bf16[8,704,256]{2,1,0:T(8,128)(2,1)S(1)}, u32[]{:S(2)}, u32[]{:S(2)}) async-start(bf16[8,704,256]{2,1,0:T(8,128)(2,1)} %fusion.102), calls=%async_computation.10 | async-start | bytes 5767168 | tf_op jit(solution)/shard_map/cond/branch_1_fun/all_to_all | solution.py:129
  335.7 1.6 copy-start.4
  337.4 69.1 %all-to-all-start.11 = ((bf16[8,704,256]{2,1,0:T(8,128)(2,1)}), bf16[8,704,256]{2,1,0:T(8,128)(2,1)S(1)}, u32[]{:S(2)}, u32[]{:S(2)}) async-start(bf16[8,704,256]{2,1,0:T(8,128)(2,1)} %fusion.103), calls=%async_computation.11 | async-start | bytes 5767168 | tf_op jit(solution)/shard_map/cond/branch_1_fun/all_to_all | solution.py:129
  406.5 69.3 %all-to-all-start.7 = ((bf16[8,704,256]{2,1,0:T(8,128)(2,1)}), bf16[8,704,256]{2,1,0:T(8,128)(2,1)}, u32[]{:S(2)}, u32[]{:S(2)}) async-start(bf16[8,704,256]{2,1,0:T(8,128)(2,1)} %fusion.99), calls=%async_computation.7 | async-start | bytes 5767168 | tf_op jit(solution)/shard_map/cond/branch_1_fun/all_to_all | solution.py:129
  475.8 69.3 %all-to-all-start.9 = ((bf16[8,704,256]{2,1,0:T(8,128)(2,1)}), bf16[8,704,256]{2,1,0:T(8,128)(2,1)S(1)}, u32[]{:S(2)}, u32[]{:S(2)}) async-start(bf16[8,704,256]{2,1,0:T(8,128)(2,1)} %fusion.101), calls=%async_computation.9 | async-start | bytes 5767168 | tf_op jit(solution)/shard_map/cond/branch_1_fun/all_to_all | solution.py:129
  479.9 24.3 %copy-start.5 = (f32[240]{0:T(256)S(1)}, f32[240]{0:T(256)}, u32[]{:S(2)}) copy-start(f32[240]{0:T(256)} %sine_multiply_fusion.1) | copy-start | bytes 2884 | tf_op jit(solution)/shard_map/conditional.1
  570.9 3.1 copy-start.3
Sparse Core Ops, SparseCore 0:
  159.9 104.1 all-gather.8
  266.2 105.0 all-gather.10

commit v3 on v2

--- a/solution.py
+++ b/solution.py
@@ -6,6 +6,7 @@
 from jax.experimental import pallas as pl
 from jax.experimental.pallas import tpu as pltpu
 from jax.sharding import PartitionSpec as P
+
 
 SPREADS = 3.5
 LANES = 128
@@ -59,8 +60,8 @@
     parity = 1.0 - 2.0 * (orders % 2).astype(jnp.float32)[:, None]
     start = parity * jnp.exp(log_start + order_real * jnp.log(sine))
 
-    level = jnp.arange(degree_range).astype(jnp.float32)[:, None, None]
-    order_wide = jnp.broadcast_to(order_real[None], (1, slots, LANES))
+    level = jnp.arange(degree_range).astype(jnp.float32)[:, None]
+    order_wide = order_real[:, 0][None, :]
     upper = jnp.sqrt(
         jnp.maximum(4.0 * level * level - 1.0, 0.0)
         / jnp.maximum(level * level - order_wide * order_wide, 1.0)
@@ -68,6 +69,10 @@
     lower = jnp.sqrt(
         jnp.maximum((level - 1.0) * (level - 1.0) - order_wide * order_wide, 0.0)
         / jnp.maximum(4.0 * (level - 1.0) * (level - 1.0) - 1.0, 1.0)
+    )
+    upper, lower = (
+        jnp.broadcast_to(lax.optimization_barrier(part)[:, :, None], part.shape + (LANES,))
+        for part in (upper, lower)
     )
     places = jnp.arange(total).astype(jnp.int32)
     degrees = jnp.arange(degree_range).astype(jnp.int32)
@@ -103,21 +108,14 @@
     return jnp.pi / latitude_count * jnp.sin(angles)
 
 
-def dense_exchange(peers, slots):
+def dense_exchange():
     def exchange(value):
-        moved = lax.all_to_all(
-            value.reshape(peers, slots, slots, value.shape[-1]),
-            "order",
-            split_axis=0,
-            concat_axis=0,
-            tiled=True,
-        )
-        return moved
+        return lax.all_to_all(value, "order", split_axis=0, concat_axis=0, tiled=True)
 
     return exchange, exchange
 
 
-def packed_exchange(peers, slots, capacity, leave, arrive):
+def packed_exchange(capacity, leave, arrive):
     place = jnp.arange(capacity).astype(jnp.int32)[None, :, None, None]
     leave_matrix = (leave[:, None] == place).astype(jnp.bfloat16)
     arrive_matrix = (arrive[:, None] == place).astype(jnp.bfloat16)
@@ -137,12 +135,24 @@
     )
 
 
-def layer(send, back, cotangent, stored_coefficients, weights, table, pick):
+def layer(exchanges, cotangent, stored_coefficients, weights, table, mine, degree_table, *ranks):
+    return layer_body(
+        exchanges(*ranks), cotangent, stored_coefficients, weights, table, mine, degree_table
+    )
+
+
+def layer_body(exchanges, cotangent, stored_coefficients, weights, table, mine, degree_table):
+    send, back = exchanges
     slots, latitude_count, batch_size, parts, width = cotangent.shape
     degree_range = stored_coefficients.shape[1]
     rows = batch_size * parts
     cot = cotangent.reshape(slots, latitude_count, rows, width)
     stored = stored_coefficients.reshape(slots, degree_range, rows, width)
+    degrees = jnp.arange(degree_range).astype(jnp.int32)
+    pick = (degree_table[:, None, None] == degrees[None, None, :]) & (
+        degrees[None, None, :] >= mine[None, :, None]
+    )
+    pick = pick.astype(jnp.bfloat16).reshape(table.shape[:3] + (degree_range,))
 
     def project(matrix, source):
         return jnp.einsum(
@@ -181,18 +191,13 @@
     owned = lax.dynamic_slice_in_dim(degree_table, position * slots, slots)
     table = picked_legendre(mine, degree_table, degree_range, latitude_count)
     table = table.reshape(peers, slots, slots, latitude_count)
-    degrees = jnp.arange(degree_range).astype(jnp.int32)
-    pick = (degree_table[:, None, None] == degrees[None, None, :]) & (
-        degrees[None, None, :] >= mine[None, :, None]
-    )
-    pick = pick.astype(jnp.bfloat16).reshape(peers, slots, slots, degree_range)
-    operands = (cotangent, stored_coefficients, weights, table, pick)
+    operands = (cotangent, stored_coefficients, weights, table, mine, degree_table)
 
     full = slots * slots
     live = degree_range * (degree_range + 1) / 2 / (peers * slots) ** 2
     spread = (full * (2 * slots + 1) / 12) ** 0.5
     capacity = -(-int(live * full + SPREADS * spread) // 16) * 16
-    dense = functools.partial(layer, *dense_exchange(peers, slots))
+    dense = functools.partial(layer, lambda *ranks: dense_exchange())
     if capacity > 0.85 * full:
         return dense(*operands)
 
@@ -212,8 +217,8 @@
         ((degree_rows >= order_rows) & (degree_rows < degree_range)).astype(jnp.int32), axis=(2, 3)
     )
     fits = jnp.max(counts) <= capacity
-    packed = functools.partial(layer, *packed_exchange(peers, slots, capacity, leave, arrive))
-    return lax.cond(fits, packed, dense, *operands)
+    packed = functools.partial(layer, functools.partial(packed_exchange, capacity))
+    return lax.cond(fits, packed, dense, *operands, leave, arrive)
 
 
 def solution(mesh):

time: 587 us -> 576 us (0.981)
  waiting for transfers between devices: 125 us -> 199 us
  blocking collectives: 140 us -> 68.9 us
  other arithmetic: 34.1 us -> 9.84 us
  starting transfers between devices: 16.4 us -> 24 us
  local copies, waits for them, and re-layouts: 34.1 us -> 40.7 us
  matrix products: 200 us -> 194 us
    all_to_all x2 -> x1, blocking collectives: 140 us -> 68.9 us  [route(): lax.all_to_all(packed, 'order', split_axis=0, concat_axis=0, tiled=True)]
    all_to_all x4 -> x5, waiting for transfers between devices: 125 us -> 192 us  [route(): lax.all_to_all(packed, 'order', split_axis=0, concat_axis=0, tiled=True)]
    convert_element_type x3 -> x0, other arithmetic: 15 us -> none  [the longest x1 6.11 us: packed_exchange(): arrive_matrix = (arrive[:, None] == place).astype(jnp.bfloat16)]
    dot_general x6, matrix products: 71.7 us -> 58 us  [route(): jnp.einsum('tpks,tksc->tpc', packer, value, preferred_element_type=jnp.fl...]
    sqrt x1, other arithmetic: 9.08 us -> 0.09 us  [picked_legendre(): jnp.sqrt(jnp.maximum((level - 1.0) * (level - 1.0) - order_wide * order_w...]
    all_to_all x4 -> x5, starting transfers between devices: 16.3 us -> 23.7 us  [route(): lax.all_to_all(packed, 'order', split_axis=0, concat_axis=0, tiled=True)]
    all_gather x2, waiting for transfers between devices: 0.01 us -> 7.14 us  [layer_body(): gathered.append(lax.all_gather(adjoint, 'chan', axis=3, tiled=True))]
    dot_general x6 -> x10, matrix products: 96.9 us -> 104 us  [the longest x2 42.9 us: layer_body(): jnp.einsum('nksc,nksd->kcd', saved[r], gathered[r], preferred_element_typ...]
  transfers between devices with their start and end apart: 6 -> 7, of which waited for: 4 -> 6; matrix products, arithmetic and copies ran while one was open for 30% -> 29% of each run, Pallas kernels for 0% -> 0%
where the time goes in v3:
time: 576 us; the launch traced here: 568 us
  waiting for transfers between devices  199 us (35%)
  matrix products  194 us (34%)
  blocking collectives  68.9 us (12%)
  local copies, waits for them, and re-layouts  40.7 us (7%)
  starting transfers between devices  24 us (4%)
  between operations  15.1 us (3%)
  other arithmetic  9.84 us (2%)
  loops' own time  8.26 us (1%)
  Pallas kernels  7.54 us (1%)
    all_to_all x5, waiting for transfers between devices, route(): lax.all_to_all(packed, 'order', split_axis=0, concat_axis=0, tiled=True)  192 us
    all_to_all x1, blocking collectives, route(): lax.all_to_all(packed, 'order', split_axis=0, concat_axis=0, tiled=True)  68.9 us
    dot_general x6, matrix products, route(): jnp.einsum('tpks,tksc->tpc', packer, value, preferred_element_type=jnp.fl...  58 us
    dot_general x2, matrix products, layer_body(): jnp.einsum('nksc,nksd->kcd', saved[r], gathered[r], preferred_element_typ...  42.9 us
    dot_general x5, matrix products, route(): jnp.einsum('tpks,tpc->tksc', unpacker, moved, preferred_element_type=jnp....  30.6 us
    dot_general x2, matrix products, layer_body(): jnp.einsum('nksd,kcd->nksc', gathered[r], weights, preferred_element_type...  27.5 us
    another operation x33, local copies, waits for them, and re-layouts  26.6 us
    all_to_all x5, starting transfers between devices, route(): lax.all_to_all(packed, 'order', split_axis=0, concat_axis=0, tiled=True)  23.7 us
  transfers between devices with their start and end apart: 7, of which 6 were waited for; matrix products, arithmetic and copies ran while one was open for 29% of the time, Pallas kernels for 0%

profile of v3, /device:TPU:0, one launch (start us, length us, event | category | flops | bytes accessed | tf_op | source)
XLA Modules:
  0.0 567.8 jit_solution(5778552190351476173)
XLA Ops:
  7.2 0.8 select_reduce_fusion
  8.0 0.6 broadcast_minimum_fusion.where_ref
  8.7 0.8 fusion.181
  9.7 0.8 broadcast_compare_fusion.1
  10.4 0.8 ge.105
  11.2 0.8 ge.107
  12.0 0.5 convert_reduce_fusion
  12.5 0.6 reduce_max.9
  14.3 0.7 broadcast_in_dim.29.order_ref
  15.0 0.7 exponential_multiply_fusion.start_ref
  15.9 0.6 broadcast_in_dim.30.cosine_ref
  17.1 0.5 copy-done.12
  17.6 0.9 fusion.163
  18.6 0.9 fusion.164
  19.6 2.5 broadcast_in_dim.28.lower_ref
  22.0 2.5 broadcast_in_dim.27.upper_ref
  24.5 7.5 %legendre.1 = bf16[248,31,240]{2,1,0:T(8,128)(2,1)} custom-call(s32[240]{0:T(256)} %broadcast_minimum_fusion.where_ref, f32[240,31,128]{2,1,0:T(8,128)} %broadcast_in_dim.27.upper_ref, f32[240,31,128]{2,1,0:T(8,128)} %broadcast_in_dim.28.lower_ref, s32[31,128]{1,0:T(8,128)} %broadcast_in_dim.29.order_ref, f32[31,240]{1,0:T(8,128)} %broadcast_in_dim.30.cosine_ref, ...), custom_call_target="tpu_custom_call" | custom-call | flops 10713600 | bytes 25165824 | tf_op jit(solution)/shard_map/legendre/pallas_call | solution.py:85
  32.1 525.4 %conditional.2 = (bf16[31,256,1024]{2,1,0:T(8,128)(2,1)}, bf16[31,240,1,2,256]{4,3,2,1,0:T(2,128)(2,1)S(1)}) conditional(s32[]{:T(128)} %convert_element_type.233, (bf16[31,240,1,2,256]{4,3,2,1,0:T(2,128)(2,1)}, bf16[8,31,31,240]{3,2,1,0:T(8,128)(2,1)}, bf16[31,256,1024]{2,1,0:T(8,128)(2,1)}, s32[248]{0:T(256)S(1)}, s32[31]{0:T(128)S(1)}, ...), branch_computations={%region_4.5_spmd, %region_5.6_spmd} | conditional | flops 55165427712 | bytes 676317376
  39.9 0.6 copy-done.19
  40.5 0.9 reshape.241
  41.4 0.9 and_select_fusion.1
  42.5 7.6 %copy.241 = bf16[31,240,1,2,256]{4,1,0,3,2:T(8,128)(2,1)} copy(bf16[31,240,1,2,256]{4,3,2,1,0:T(2,128)(2,1)} %get-tuple-element.178) | data formatting | bytes 15237120 | tf_op jit(solution)/shard_map
  50.1 6.7 %convert_bitcast_fusion.8 = bf16[8,31,31,256]{3,1,0,2:T(8,128)(2,1)S(1)} fusion(bf16[31,240,2,256]{3,1,0,2:T(8,128)(2,1)} %bitcast.248, bf16[8,31,31,240]{3,2,1,0:T(8,128)(2,1)S(1)} %copy-done.1), kind=kOutput, calls=%fused_computation.116 | convolution fusion | flops 946669568 | bytes 11435776 | tf_op jit(solution)/shard_map/cond/branch_1_fun/tksj,sjc->tksc/dot_general | solution.py:158
  56.7 9.6 %bitcast_convert_fusion.3 = bf16[8,704,256]{2,1,0:T(8,128)(2,1)} fusion(bf16[8,31,31,256]{3,1,0,2:T(8,128)(2,1)S(1)} %convert_bitcast_fusion.8, s32[8,31,31]{1,2,0:T(8,128)S(1)} %copy.114), kind=kOutput, calls=%fused_computation.100 | convolution fusion | flops 2777978368 | bytes 6850592 | tf_op jit(solution)/shard_map/cond/branch_1_fun/tpks,tksc->tpc/dot_general | solution.py:124
  66.3 7.4 %all-to-all-start.8 = ((bf16[8,704,256]{2,1,0:T(8,128)(2,1)}), bf16[8,704,256]{2,1,0:T(8,128)(2,1)S(1)}, u32[]{:S(2)}, u32[]{:S(2)}) async-start(bf16[8,704,256]{2,1,0:T(8,128)(2,1)} %bitcast_convert_fusion.3), calls=%async_computation.8 | async-start | bytes 5767168 | tf_op jit(solution)/shard_map/cond/branch_1_fun/all_to_all | solution.py:127
  74.1 64.7 %all-to-all-done.8 = bf16[8,704,256]{2,1,0:T(8,128)(2,1)S(1)} async-done(((bf16[8,704,256]{2,1,0:T(8,128)(2,1)}), bf16[8,704,256]{2,1,0:T(8,128)(2,1)S(1)}, u32[]{:S(2)}, u32[]{:S(2)}) %all-to-all-start.8) | async-done | bytes 2883616 | tf_op jit(solution)/shard_map/cond/branch_1_fun/all_to_all | solution.py:127
  138.8 5.7 %fusion.128 = bf16[8,31,31,256]{3,2,1,0:T(8,128)(2,1)} fusion(bf16[8,704,256]{2,1,0:T(8,128)(2,1)S(1)} %all-to-all-done.8, s32[8,31,31]{2,0,1:T(8,128)S(1)} %copy.115), kind=kOutput, calls=%fused_computation.140 | convolution fusion | flops 2778504704 | bytes 6850592 | tf_op jit(solution)/shard_map/cond/branch_1_fun/tpks,tpc->tksc/dot_general | solution.py:128
  144.5 0.2 all-gather.9.cloned.1.call-start
  144.8 7.8 %convert_bitcast_fusion.9 = bf16[8,31,31,256]{3,1,0,2:T(8,128)(2,1)S(1)} fusion(bf16[31,240,2,256]{3,1,0,2:T(8,128)(2,1)} %bitcast.249, bf16[8,31,31,240]{3,2,1,0:T(8,128)(2,1)} %get-tuple-element.179), kind=kOutput, calls=%fused_computation.120 | convolution fusion | flops 946669568 | bytes 11808768 | tf_op jit(solution)/shard_map/cond/branch_1_fun/tksj,sjc->tksc/dot_general | solution.py:158
  152.6 8.7 %bitcast_convert_fusion.5 = bf16[8,704,256]{2,1,0:T(8,128)(2,1)S(1)} fusion(bf16[8,31,31,256]{3,1,0,2:T(8,128)(2,1)S(1)} %convert_bitcast_fusion.9, s32[8,31,31]{1,2,0:T(8,128)S(1)} %copy.114), kind=kOutput, calls=%fused_computation.102 | convolution fusion | flops 2777978368 | bytes 6850592 | tf_op jit(solution)/shard_map/cond/branch_1_fun/tpks,tksc->tpc/dot_general | solution.py:124
  161.3 68.9 %all_to_all.50 = bf16[8,704,256]{2,1,0:T(8,128)(2,1)S(1)} all-to-all(bf16[8,704,256]{2,1,0:T(8,128)(2,1)S(1)} %bitcast_convert_fusion.5), channel_id=1, replica_groups=mesh['order'=8,'chan'=4] {'order'}, dimensions={0} | all-to-all | bytes 5767168 | tf_op jit(solution)/shard_map/cond/branch_1_fun/all_to_all | solution.py:127
  230.2 5.7 %fusion.123 = bf16[8,31,31,256]{3,2,1,0:T(8,128)(2,1)} fusion(bf16[8,704,256]{2,1,0:T(8,128)(2,1)S(1)} %all_to_all.50, s32[8,31,31]{2,0,1:T(8,128)S(1)} %copy.115), kind=kOutput, calls=%fused_computation.139 | convolution fusion | flops 2778504704 | bytes 6850592 | tf_op jit(solution)/shard_map/cond/branch_1_fun/tpks,tpc->tksc/dot_general | solution.py:128
  235.9 0.7 copy-done.20
  236.7 4.3 copy.240
  241.2 1.3 convert_bitcast_fusion.7
  242.4 1.7 copy-done.6
  244.1 9.5 %bitcast_convert_fusion.1 = bf16[8,704,256]{2,1,0:T(8,128)(2,1)} fusion(bf16[8,31,31,256]{3,1,0,2:T(8,128)(2,1)S(1)} %convert_bitcast_fusion.7, s32[8,31,31]{1,2,0:T(8,128)S(1)} %copy.114), kind=kOutput, calls=%fused_computation.98 | convolution fusion | flops 2777978368 | bytes 6850592 | tf_op jit(solution)/shard_map/cond/branch_1_fun/tpks,tksc->tpc/dot_general | solution.py:124
  253.6 3.7 all-to-all-start.10
  257.3 0.6 sine_multiply_fusion.1
  258.0 4.0 convert_bitcast_fusion.6
  262.0 9.5 %bitcast_convert_fusion = bf16[8,704,256]{2,1,0:T(8,128)(2,1)} fusion(bf16[8,31,31,256]{3,1,0,2:T(8,128)(2,1)S(1)} %convert_bitcast_fusion.6, s32[8,31,31]{1,2,0:T(8,128)S(1)} %copy.114), kind=kOutput, calls=%fused_computation.97 | convolution fusion | flops 2777978368 | bytes 6850592 | tf_op jit(solution)/shard_map/cond/branch_1_fun/tpks,tksc->tpc/dot_general | solution.py:124
  271.5 50.6 %all-to-all-done.10 = bf16[8,704,256]{2,1,0:T(8,128)(2,1)S(1)} async-done(((bf16[8,704,256]{2,1,0:T(8,128)(2,1)}), bf16[8,704,256]{2,1,0:T(8,128)(2,1)S(1)}, u32[]{:S(2)}, u32[]{:S(2)}) %all-to-all-start.10) | async-done | bytes 2883616 | tf_op jit(solution)/shard_map/cond/branch_1_fun/all_to_all | solution.py:127
  322.1 1.6 copy-done.9
  323.7 3.9 all-to-all-start.11
  327.6 7.1 %fusion.197 = bf16[8,31,31,256]{3,2,0,1:T(8,128)(2,1)} fusion(s32[8,31,31]{2,0,1:T(8,128)S(1)} %copy.115, bf16[8,704,256]{2,1,0:T(8,128)(2,1)} %copy-done.9), kind=kOutput, calls=%fused_computation.111.clone.1 | convolution fusion | flops 2778504704 | bytes 6850592 | tf_op jit(solution)/shard_map/cond/branch_1_fun/tpks,tpc->tksc/dot_general | solution.py:128
  334.8 13.7 %fusion.64 = bf16[31,8,31,256]{3,2,1,0:T(8,128)(2,1)} fusion(bf16[31,256,1024]{2,1,0:T(8,128)(2,1)} %get-tuple-element.73, bf16[8,31,31,1024]{3,2,1,0:T(8,128)(2,1)} %all-gather.11.cloned.1.call-done), kind=kOutput, calls=%fused_computation.68 | convolution fusion | flops 4030726144 | bytes 35934208 | tf_op jit(solution)/shard_map/cond/branch_1_fun/nksd,kcd->nksc/dot_general | solution.py:170
  348.4 7.1 %all-gather.9.cloned.1.call-done = bf16[8,31,31,1024]{3,2,1,0:T(8,128)(2,1)} async-done(((bf16[8,31,31,256]{3,2,1,0:T(8,128)(2,1)}), bf16[8,31,31,1024]{3,2,1,0:T(8,128)(2,1)}) %all-gather.9.cloned.1.call-update) | async-done | bytes 15745040 | tf_op jit(solution)/shard_map/cond/branch_1_fun/all_gather | solution.py:165
  355.6 13.8 %fusion.66 = bf16[31,8,31,256]{3,2,1,0:T(8,128)(2,1)} fusion(bf16[31,256,1024]{2,1,0:T(8,128)(2,1)} %get-tuple-element.73, bf16[8,31,31,1024]{3,2,1,0:T(8,128)(2,1)} %all-gather.9.cloned.1.call-done), kind=kOutput, calls=%fused_computation.70 | convolution fusion | flops 4030726144 | bytes 35934208 | tf_op jit(solution)/shard_map/cond/branch_1_fun/nksd,kcd->nksc/dot_general | solution.py:170
  369.4 9.6 %bitcast_convert_fusion.2 = bf16[8,704,256]{2,1,0:T(8,128)(2,1)} fusion(bf16[31,8,31,256]{3,2,1,0:T(8,128)(2,1)S(1)} %copy-done.26, s32[8,31,31]{2,0,1:T(8,128)S(1)} %copy.115), kind=kOutput, calls=%fused_computation.99 | convolution fusion | flops 2777978368 | bytes 6850592 | tf_op jit(solution)/shard_map/cond/branch_1_fun/tpks,tksc->tpc/dot_general | solution.py:124
  379.0 13.9 %all-to-all-done.11 = bf16[8,704,256]{2,1,0:T(8,128)(2,1)S(1)} async-done(((bf16[8,704,256]{2,1,0:T(8,128)(2,1)}), bf16[8,704,256]{2,1,0:T(8,128)(2,1)S(1)}, u32[]{:S(2)}, u32[]{:S(2)}) %all-to-all-start.11) | async-done | bytes 2883616 | tf_op jit(solution)/shard_map/cond/branch_1_fun/all_to_all | solution.py:127
  392.9 4.9 all-to-all-start.9
  397.7 11.1 %bitcast_convert_fusion.4 = bf16[8,704,256]{2,1,0:T(8,128)(2,1)} fusion(bf16[31,8,31,256]{3,2,1,0:T(8,128)(2,1)} %fusion.66, s32[8,31,31]{2,0,1:T(8,128)S(1)} %copy.115), kind=kOutput, calls=%fused_computation.101 | convolution fusion | flops 2777978368 | bytes 6850592 | tf_op jit(solution)/shard_map/cond/branch_1_fun/tpks,tksc->tpc/dot_general | solution.py:124
  408.8 18.6 %fusion.68 = f32[31,256,1024,1]{2,1,3,0:T(8,128)} fusion(bf16[8,31,31,1024]{3,2,1,0:T(8,128)(2,1)} %all-gather.11.cloned.1.call-done, s32[8,31,31]{2,0,1:T(8,128)S(1)} %copy.115, bf16[8,704,256]{2,1,0:T(8,128)(2,1)S(1)} %all-to-all-done.11), kind=kOutput, calls=%fused_computation.72 | convolution fusion | flops 6809230848 | bytes 51165216 | tf_op jit(solution)/shard_map/cond/branch_1_fun/nksc,nksd->kcd/dot_general | solution.py:179
  427.4 34.9 %all-to-all-done.9 = bf16[8,704,256]{2,1,0:T(8,128)(2,1)} async-done(((bf16[8,704,256]{2,1,0:T(8,128)(2,1)}), bf16[8,704,256]{2,1,0:T(8,128)(2,1)}, u32[]{:S(2)}, u32[]{:S(2)}) %all-to-all-start.9) | async-done | bytes 2883616 | tf_op jit(solution)/shard_map/cond/branch_1_fun/all_to_all | solution.py:127
  462.4 3.8 all-to-all-start.7
  466.2 24.3 %fusion.47 = bf16[31,256,1024]{2,1,0:T(8,128)(2,1)} fusion(f32[31,256,1024,1]{2,1,3,0:T(8,128)} %fusion.68, bf16[8,31,31,1024]{3,2,1,0:T(8,128)(2,1)} %all-gather.9.cloned.1.call-done, bf16[8,31,31,256]{3,2,0,1:T(8,128)(2,1)} %fusion.197), kind=kOutput, calls=%fused_computation.49 | convolution fusion | flops 4046979072 | bytes 68440064 | tf_op jit(solution)/shard_map/cond/branch_1_fun/nksc,nksd->kcd/dot_general | solution.py:179
  490.5 6.1 %fusion.56 = bf16[8,31,31,256]{3,1,0,2:T(8,128)(2,1)S(1)} fusion(bf16[8,704,256]{2,1,0:T(8,128)(2,1)} %all-to-all-done.9, s32[8,31,31]{1,2,0:T(8,128)S(1)} %copy-done.16), kind=kOutput, calls=%fused_computation.60 | convolution fusion | flops 2776536576 | bytes 6850592 | tf_op jit(solution)/shard_map/cond/branch_1_fun/tpks,tpc->tksc/dot_general | solution.py:128
  496.6 7.0 %fusion.109 = bf16[31,240,1,256]{3,1,0,2:T(8,128)(2,1)} fusion(f32[240]{0:T(256)S(1)} %copy-done.25, bf16[8,31,31,240]{3,2,1,0:T(8,128)(2,1)S(1)} %copy-done.2, bf16[8,31,31,256]{3,1,0,2:T(8,128)(2,1)S(1)} %fusion.56), kind=kOutput, calls=%fused_computation.126 | convolution fusion | flops 948510720 | bytes 11436736 | tf_op jit(solution)/shard_map/cond/branch_1_fun/tksj,tksc->sjc/dot_general | solution.py:173
  503.6 27.8 %all-to-all-done.7 = bf16[8,704,256]{2,1,0:T(8,128)(2,1)S(1)} async-done(((bf16[8,704,256]{2,1,0:T(8,128)(2,1)}), bf16[8,704,256]{2,1,0:T(8,128)(2,1)S(1)}, u32[]{:S(2)}, u32[]{:S(2)}) %all-to-all-start.7) | async-done | bytes 2883616 | tf_op jit(solution)/shard_map/cond/branch_1_fun/all_to_all | solution.py:127
  531.4 6.0 %fusion.58 = bf16[8,31,31,256]{3,1,0,2:T(8,128)(2,1)S(1)} fusion(bf16[8,704,256]{2,1,0:T(8,128)(2,1)S(1)} %all-to-all-done.7, s32[8,31,31]{1,2,0:T(8,128)S(1)} %copy-done.16), kind=kOutput, calls=%fused_computation.62 | convolution fusion | flops 2776536576 | bytes 6850592 | tf_op jit(solution)/shard_map/cond/branch_1_fun/tpks,tpc->tksc/dot_general | solution.py:128
  537.4 6.9 %fusion.108 = bf16[31,240,1,256]{3,1,0,2:T(8,128)(2,1)} fusion(f32[240]{0:T(256)S(1)} %copy-done.25, bf16[8,31,31,240]{3,2,1,0:T(8,128)(2,1)S(1)} %copy-done.3, bf16[8,31,31,256]{3,1,0,2:T(8,128)(2,1)S(1)} %fusion.58), kind=kOutput, calls=%fused_computation.125 | convolution fusion | flops 948510720 | bytes 11436736 | tf_op jit(solution)/shard_map/cond/branch_1_fun/tksj,tksc->sjc/dot_general | solution.py:173
  544.4 2.8 maximum_bitcast_fusion.1
  547.2 10.1 %copy.160 = bf16[31,240,1,2,256]{4,3,2,1,0:T(2,128)(2,1)S(1)} copy(bf16[31,240,1,2,256]{4,1,0,3,2:T(8,128)(2,1)S(1)} %maximum_bitcast_fusion.1) | data formatting | bytes 15237120 | tf_op jit(solution)/shard_map/conditional
  557.5 3.1 copy-done.8
  (78 shorter events, 2.5 us)
Async XLA Ops:
  10.4 3.5 copy-start.21
  10.4 4.5 copy-start.23
  15.7 1.0 copy-start.13
  16.9 0.7 copy-start.12
  24.5 7.6 %copy-start.14 = (pred[8,31,31]{2,1,0:T(8,128)(4,1)S(1)}, pred[8,31,31]{2,1,0:T(8,128)(4,1)}, u32[]{:S(2)}) copy-start(pred[8,31,31]{2,1,0:T(8,128)(4,1)} %copy-done.13) | copy-start | bytes 23068
  24.5 7.6 %copy-start.18 = (s32[248]{0:T(256)S(1)}, s32[248]{0:T(256)}, u32[]{:S(2)}) copy-start(s32[248]{0:T(256)} %param.11) | copy-start | bytes 2980
  24.5 7.6 %copy-start.22 = (pred[31]{0:T(512)(128)(4,1)S(1)}, pred[31]{0:T(512)(128)(4,1)}, u32[]{:S(2)}) copy-start(pred[31]{0:T(512)(128)(4,1)} %copy-done.21) | copy-start | bytes 97
  24.5 7.6 %copy-start.24 = (s32[31]{0:T(128)S(1)}, s32[31]{0:T(128)}, u32[]{:S(2)}) copy-start(s32[31]{0:T(128)} %copy-done.23) | copy-start | bytes 376
  39.9 0.6 copy-start.19
  40.5 9.6 %copy-start.10 = (s32[8,31,31]{2,1,0:T(8,128)}, s32[8,31,31]{2,1,0:T(8,128)S(1)}, u32[]{:S(2)}) copy-start(s32[8,31,31]{2,1,0:T(8,128)S(1)} %get-tuple-element.68) | copy-start | bytes 92260 | tf_op jit(solution)/shard_map/conditional
  42.5 219.5 %copy-start.15 = (s32[8,31,31]{1,2,0:T(8,128)}, s32[8,31,31]{1,2,0:T(8,128)S(1)}, u32[]{:S(2)}) copy-start(s32[8,31,31]{1,2,0:T(8,128)S(1)} %copy.114) | copy-start | bytes 92260 | tf_op jit(solution)/shard_map/conditional
  42.5 7.6 %copy-start.1 = (bf16[8,31,31,240]{3,2,1,0:T(8,128)(2,1)S(1)}, bf16[8,31,31,240]{3,2,1,0:T(8,128)(2,1)}, u32[]{:S(2)}) copy-start(bf16[8,31,31,240]{3,2,1,0:T(8,128)(2,1)} %get-tuple-element.179) | copy-start | bytes 11070724 | tf_op jit(solution)/shard_map/conditional
  66.3 7.5 %copy-start.17 = (s32[8,961]{1,0:T(8,128)S(1)}, s32[8,961]{1,0:T(8,128)}, u32[]{:S(2)}) copy-start(s32[8,961]{1,0:T(8,128)} %get-tuple-element.70) | copy-start | bytes 92260 | tf_op jit(solution)/shard_map/conditional
  66.3 7.6 %copy-start.11 = (s32[8,31,31]{2,1,0:T(8,128)S(1)}, s32[8,31,31]{2,1,0:T(8,128)}, u32[]{:S(2)}) copy-start(s32[8,31,31]{2,1,0:T(8,128)} %copy-done.10) | copy-start | bytes 92260 | tf_op jit(solution)/shard_map/conditional
  66.3 72.5 %all-to-all-start.8 = ((bf16[8,704,256]{2,1,0:T(8,128)(2,1)}), bf16[8,704,256]{2,1,0:T(8,128)(2,1)S(1)}, u32[]{:S(2)}, u32[]{:S(2)}) async-start(bf16[8,704,256]{2,1,0:T(8,128)(2,1)} %bitcast_convert_fusion.3), calls=%async_computation.8 | async-start | bytes 5767168 | tf_op jit(solution)/shard_map/cond/branch_1_fun/all_to_all | solution.py:127
  73.7 261.0 %all-gather.11.cloned.1.call-start = ((), (), s32[]{:S(2)}) async-start(), calls=%async_computation.15 | async-start | bytes 20316160 | tf_op jit(solution)/shard_map/cond/branch_1_fun/all_gather | solution.py:165
  144.5 211.0 %all-gather.9.cloned.1.call-start = ((), (), s32[]{:S(2)}) async-start(), calls=%async_computation.14 | async-start | bytes 20316160 | tf_op jit(solution)/shard_map/cond/branch_1_fun/all_gather | solution.py:165
  235.9 0.7 copy-start.20
  241.0 3.1 copy-start.6
  253.6 68.4 %all-to-all-start.10 = ((bf16[8,704,256]{2,1,0:T(8,128)(2,1)}), bf16[8,704,256]{2,1,0:T(8,128)(2,1)S(1)}, u32[]{:S(2)}, u32[]{:S(2)}) async-start(bf16[8,704,256]{2,1,0:T(8,128)(2,1)} %bitcast_convert_fusion.1), calls=%async_computation.10 | async-start | bytes 5767168 | tf_op jit(solution)/shard_map/cond/branch_1_fun/all_to_all | solution.py:127
  322.1 1.6 copy-start.9
  323.7 69.1 %all-to-all-start.11 = ((bf16[8,704,256]{2,1,0:T(8,128)(2,1)}), bf16[8,704,256]{2,1,0:T(8,128)(2,1)S(1)}, u32[]{:S(2)}, u32[]{:S(2)}) async-start(bf16[8,704,256]{2,1,0:T(8,128)(2,1)} %bitcast_convert_fusion), calls=%async_computation.11 | async-start | bytes 5767168 | tf_op jit(solution)/shard_map/cond/branch_1_fun/all_to_all | solution.py:127
  355.6 13.8 %copy-start.26 = (bf16[31,8,31,256]{3,2,1,0:T(8,128)(2,1)S(1)}, bf16[31,8,31,256]{3,2,1,0:T(8,128)(2,1)}, u32[]{:S(2)}) copy-start(bf16[31,8,31,256]{3,2,1,0:T(8,128)(2,1)} %fusion.64) | copy-start | bytes 11808772 | tf_op jit(solution)/shard_map/conditional
  392.9 69.5 %all-to-all-start.9 = ((bf16[8,704,256]{2,1,0:T(8,128)(2,1)}), bf16[8,704,256]{2,1,0:T(8,128)(2,1)}, u32[]{:S(2)}, u32[]{:S(2)}) async-start(bf16[8,704,256]{2,1,0:T(8,128)(2,1)} %bitcast_convert_fusion.2), calls=%async_computation.9 | async-start | bytes 5767168 | tf_op jit(solution)/shard_map/cond/branch_1_fun/all_to_all | solution.py:127
  462.4 69.1 %all-to-all-start.7 = ((bf16[8,704,256]{2,1,0:T(8,128)(2,1)}), bf16[8,704,256]{2,1,0:T(8,128)(2,1)S(1)}, u32[]{:S(2)}, u32[]{:S(2)}) async-start(bf16[8,704,256]{2,1,0:T(8,128)(2,1)} %bitcast_convert_fusion.4), calls=%async_computation.7 | async-start | bytes 5767168 | tf_op jit(solution)/shard_map/cond/branch_1_fun/all_to_all | solution.py:127
  466.2 24.3 %copy-start.16 = (s32[8,31,31]{1,2,0:T(8,128)S(1)}, s32[8,31,31]{1,2,0:T(8,128)}, u32[]{:S(2)}) copy-start(s32[8,31,31]{1,2,0:T(8,128)} %copy-done.15) | copy-start | bytes 92260 | tf_op jit(solution)/shard_map/conditional
  490.5 6.1 %copy-start.2 = (bf16[8,31,31,240]{3,2,1,0:T(8,128)(2,1)S(1)}, bf16[8,31,31,240]{3,2,1,0:T(8,128)(2,1)}, u32[]{:S(2)}) copy-start(bf16[8,31,31,240]{3,2,1,0:T(8,128)(2,1)} %get-tuple-element.179) | copy-start | bytes 11070724 | tf_op jit(solution)/shard_map/conditional
  490.5 6.1 %copy-start.25 = (f32[240]{0:T(256)S(1)}, f32[240]{0:T(256)}, u32[]{:S(2)}) copy-start(f32[240]{0:T(256)} %sine_multiply_fusion.1) | copy-start | bytes 2884 | tf_op jit(solution)/shard_map/conditional
  531.4 6.0 %copy-start.3 = (bf16[8,31,31,240]{3,2,1,0:T(8,128)(2,1)S(1)}, bf16[8,31,31,240]{3,2,1,0:T(8,128)(2,1)}, u32[]{:S(2)}) copy-start(bf16[8,31,31,240]{3,2,1,0:T(8,128)(2,1)} %get-tuple-element.179) | copy-start | bytes 11070724 | tf_op jit(solution)/shard_map/conditional
  537.4 7.0 %copy-start.4 = (bf16[31,240,1,256]{3,1,0,2:T(8,128)(2,1)S(1)}, bf16[31,240,1,256]{3,1,0,2:T(8,128)(2,1)}, u32[]{:S(2)}) copy-start(bf16[31,240,1,256]{3,1,0,2:T(8,128)(2,1)} %fusion.109) | copy-start | bytes 11427844 | tf_op jit(solution)/shard_map/conditional
  557.5 3.1 copy-start.8
Sparse Core Ops, SparseCore 0:
  144.7 104.1 all-gather.10
  250.4 105.0 all-gather.8

commit v4 on v3

--- a/solution.py
+++ b/solution.py
@@ -8,7 +8,7 @@
 from jax.sharding import PartitionSpec as P
 
 
-SPREADS = 3.5
+SPREADS = 3.0
 LANES = 128
 
 
@@ -170,9 +170,8 @@
         coefficient = jnp.einsum(
             "nksd,kcd->nksc", gathered[r], weights, preferred_element_type=jnp.float32
         ).astype(jnp.bfloat16)
-        summed = jnp.einsum(
-            "tksj,tksc->sjc", table, back(coefficient), preferred_element_type=jnp.float32
-        )
+        returned = back(coefficient)
+        summed = jnp.einsum("tksj,tksc->sjc", table, returned, preferred_element_type=jnp.float32)
         outputs.append((summed * quad[None, :, None]).astype(jnp.bfloat16))
     for r in range(rows):
         mixing.append(

time: 576 us -> 559 us (0.970)
  waiting for transfers between devices: 199 us -> 185 us
    all_to_all x5, waiting for transfers between devices: 192 us -> 172 us  [route(): lax.all_to_all(packed, 'order', split_axis=0, concat_axis=0, tiled=True)]
    all_gather x2, waiting for transfers between devices: 7.14 us -> 12.9 us  [layer_body(): gathered.append(lax.all_gather(adjoint, 'chan', axis=3, tiled=True))]
  transfers between devices with their start and end apart: 7 -> 7, of which waited for: 6 -> 6; matrix products, arithmetic and copies ran while one was open for 29% -> 30% of each run, Pallas kernels for 0% -> 0%
where the time goes in v4:
time: 559 us; the launch traced here: 551 us
  matrix products  194 us (35%)
  waiting for transfers between devices  185 us (33%)
  blocking collectives  66.4 us (12%)
  local copies, waits for them, and re-layouts  40.7 us (7%)
  starting transfers between devices  23.9 us (4%)
  between operations  15.1 us (3%)
  other arithmetic  9.84 us (2%)
  loops' own time  8.23 us (1%)
  Pallas kernels  7.54 us (1%)
    all_to_all x5, waiting for transfers between devices, route(): lax.all_to_all(packed, 'order', split_axis=0, concat_axis=0, tiled=True)  172 us
    all_to_all x1, blocking collectives, route(): lax.all_to_all(packed, 'order', split_axis=0, concat_axis=0, tiled=True)  66.4 us
    dot_general x6, matrix products, route(): jnp.einsum('tpks,tksc->tpc', packer, value, preferred_element_type=jnp.fl...  57.4 us
    dot_general x2, matrix products, layer_body(): jnp.einsum('nksc,nksd->kcd', saved[r], gathered[r], preferred_element_typ...  42.9 us
    dot_general x5, matrix products, route(): jnp.einsum('tpks,tpc->tksc', unpacker, moved, preferred_element_type=jnp....  30.6 us
    dot_general x2, matrix products, layer_body(): jnp.einsum('nksd,kcd->nksc', gathered[r], weights, preferred_element_type...  27.5 us
    another operation x33, local copies, waits for them, and re-layouts  26.6 us
    all_to_all x5, starting transfers between devices, route(): lax.all_to_all(packed, 'order', split_axis=0, concat_axis=0, tiled=True)  23.7 us
  transfers between devices with their start and end apart: 7, of which 6 were waited for; matrix products, arithmetic and copies ran while one was open for 30% of the time, Pallas kernels for 0%

profile of v4, /device:TPU:0, one launch (start us, length us, event | category | flops | bytes accessed | tf_op | source)
XLA Modules:
  0.0 550.6 jit_solution(4539869242756213616)
XLA Ops:
  7.2 0.8 select_reduce_fusion
  8.0 0.6 broadcast_minimum_fusion.where_ref
  8.7 0.8 fusion.181
  9.7 0.8 broadcast_compare_fusion.1
  10.4 0.8 ge.105
  11.2 0.8 ge.107
  12.0 0.5 convert_reduce_fusion
  12.5 0.6 reduce_max.9
  14.3 0.7 broadcast_in_dim.29.order_ref
  15.0 0.7 exponential_multiply_fusion.start_ref
  15.9 0.6 broadcast_in_dim.30.cosine_ref
  17.1 0.5 copy-done.12
  17.6 0.9 fusion.163
  18.6 0.9 fusion.164
  19.6 2.5 broadcast_in_dim.28.lower_ref
  22.0 2.5 broadcast_in_dim.27.upper_ref
  24.5 7.5 %legendre.1 = bf16[248,31,240]{2,1,0:T(8,128)(2,1)} custom-call(s32[240]{0:T(256)} %broadcast_minimum_fusion.where_ref, f32[240,31,128]{2,1,0:T(8,128)} %broadcast_in_dim.27.upper_ref, f32[240,31,128]{2,1,0:T(8,128)} %broadcast_in_dim.28.lower_ref, s32[31,128]{1,0:T(8,128)} %broadcast_in_dim.29.order_ref, f32[31,240]{1,0:T(8,128)} %broadcast_in_dim.30.cosine_ref, ...), custom_call_target="tpu_custom_call" | custom-call | flops 10713600 | bytes 25165824 | tf_op jit(solution)/shard_map/legendre/pallas_call | solution.py:85
  32.1 508.3 %conditional.2 = (bf16[31,256,1024]{2,1,0:T(8,128)(2,1)}, bf16[31,240,1,2,256]{4,3,2,1,0:T(2,128)(2,1)S(1)}) conditional(s32[]{:T(128)} %convert_element_type.233, (bf16[31,240,1,2,256]{4,3,2,1,0:T(2,128)(2,1)}, bf16[8,31,31,240]{3,2,1,0:T(8,128)(2,1)}, bf16[31,256,1024]{2,1,0:T(8,128)(2,1)}, s32[248]{0:T(256)S(1)}, s32[31]{0:T(128)S(1)}, ...), branch_computations={%region_4.5_spmd, %region_5.6_spmd} | conditional | flops 53650563072 | bytes 671992000
  39.8 0.6 copy-done.19
  40.4 0.9 reshape.241
  41.3 0.9 and_select_fusion.1
  42.4 7.6 %copy.241 = bf16[31,240,1,2,256]{4,1,0,3,2:T(8,128)(2,1)} copy(bf16[31,240,1,2,256]{4,3,2,1,0:T(2,128)(2,1)} %get-tuple-element.178) | data formatting | bytes 15237120 | tf_op jit(solution)/shard_map
  50.0 6.7 %convert_bitcast_fusion.8 = bf16[8,31,31,256]{3,1,0,2:T(8,128)(2,1)S(1)} fusion(bf16[31,240,2,256]{3,1,0,2:T(8,128)(2,1)} %bitcast.248, bf16[8,31,31,240]{3,2,1,0:T(8,128)(2,1)S(1)} %copy-done.1), kind=kOutput, calls=%fused_computation.116 | convolution fusion | flops 946669568 | bytes 11435776 | tf_op jit(solution)/shard_map/cond/branch_1_fun/tksj,sjc->tksc/dot_general | solution.py:158
  56.7 9.5 %bitcast_convert_fusion.3 = bf16[8,672,256]{2,1,0:T(8,128)(2,1)} fusion(bf16[8,31,31,256]{3,1,0,2:T(8,128)(2,1)S(1)} %convert_bitcast_fusion.8, s32[8,31,31]{1,2,0:T(8,128)S(1)} %copy.114), kind=kOutput, calls=%fused_computation.100 | convolution fusion | flops 2651706624 | bytes 6719520 | tf_op jit(solution)/shard_map/cond/branch_1_fun/tpks,tksc->tpc/dot_general | solution.py:124
  66.2 7.4 %all-to-all-start.8 = ((bf16[8,672,256]{2,1,0:T(8,128)(2,1)}), bf16[8,672,256]{2,1,0:T(8,128)(2,1)S(1)}, u32[]{:S(2)}, u32[]{:S(2)}) async-start(bf16[8,672,256]{2,1,0:T(8,128)(2,1)} %bitcast_convert_fusion.3), calls=%async_computation.8 | async-start | bytes 5505024 | tf_op jit(solution)/shard_map/cond/branch_1_fun/all_to_all | solution.py:127
  74.0 61.9 %all-to-all-done.8 = bf16[8,672,256]{2,1,0:T(8,128)(2,1)S(1)} async-done(((bf16[8,672,256]{2,1,0:T(8,128)(2,1)}), bf16[8,672,256]{2,1,0:T(8,128)(2,1)S(1)}, u32[]{:S(2)}, u32[]{:S(2)}) %all-to-all-start.8) | async-done | bytes 2752544 | tf_op jit(solution)/shard_map/cond/branch_1_fun/all_to_all | solution.py:127
  135.9 5.7 %fusion.128 = bf16[8,31,31,256]{3,2,1,0:T(8,128)(2,1)} fusion(bf16[8,672,256]{2,1,0:T(8,128)(2,1)S(1)} %all-to-all-done.8, s32[8,31,31]{2,0,1:T(8,128)S(1)} %copy.115), kind=kOutput, calls=%fused_computation.140 | convolution fusion | flops 2652298496 | bytes 6719520 | tf_op jit(solution)/shard_map/cond/branch_1_fun/tpks,tpc->tksc/dot_general | solution.py:128
  141.6 0.2 all-gather.9.cloned.1.call-start
  141.8 7.8 %convert_bitcast_fusion.9 = bf16[8,31,31,256]{3,1,0,2:T(8,128)(2,1)S(1)} fusion(bf16[31,240,2,256]{3,1,0,2:T(8,128)(2,1)} %bitcast.249, bf16[8,31,31,240]{3,2,1,0:T(8,128)(2,1)} %get-tuple-element.179), kind=kOutput, calls=%fused_computation.120 | convolution fusion | flops 946669568 | bytes 11808768 | tf_op jit(solution)/shard_map/cond/branch_1_fun/tksj,sjc->tksc/dot_general | solution.py:158
  149.6 8.6 %bitcast_convert_fusion.5 = bf16[8,672,256]{2,1,0:T(8,128)(2,1)S(1)} fusion(bf16[8,31,31,256]{3,1,0,2:T(8,128)(2,1)S(1)} %convert_bitcast_fusion.9, s32[8,31,31]{1,2,0:T(8,128)S(1)} %copy.114), kind=kOutput, calls=%fused_computation.102 | convolution fusion | flops 2651706624 | bytes 6719520 | tf_op jit(solution)/shard_map/cond/branch_1_fun/tpks,tksc->tpc/dot_general | solution.py:124
  158.3 66.4 %all_to_all.50 = bf16[8,672,256]{2,1,0:T(8,128)(2,1)S(1)} all-to-all(bf16[8,672,256]{2,1,0:T(8,128)(2,1)S(1)} %bitcast_convert_fusion.5), channel_id=1, replica_groups=mesh['order'=8,'chan'=4] {'order'}, dimensions={0} | all-to-all | bytes 5505024 | tf_op jit(solution)/shard_map/cond/branch_1_fun/all_to_all | solution.py:127
  224.7 5.7 %fusion.123 = bf16[8,31,31,256]{3,2,1,0:T(8,128)(2,1)} fusion(bf16[8,672,256]{2,1,0:T(8,128)(2,1)S(1)} %all_to_all.50, s32[8,31,31]{2,0,1:T(8,128)S(1)} %copy.115), kind=kOutput, calls=%fused_computation.139 | convolution fusion | flops 2652298496 | bytes 6719520 | tf_op jit(solution)/shard_map/cond/branch_1_fun/tpks,tpc->tksc/dot_general | solution.py:128
  230.4 0.7 copy-done.20
  231.2 4.3 copy.240
  235.7 1.3 convert_bitcast_fusion.7
  236.9 1.7 copy-done.6
  238.6 9.4 %bitcast_convert_fusion.1 = bf16[8,672,256]{2,1,0:T(8,128)(2,1)} fusion(bf16[8,31,31,256]{3,1,0,2:T(8,128)(2,1)S(1)} %convert_bitcast_fusion.7, s32[8,31,31]{1,2,0:T(8,128)S(1)} %copy.114), kind=kOutput, calls=%fused_computation.98 | convolution fusion | flops 2651706624 | bytes 6719520 | tf_op jit(solution)/shard_map/cond/branch_1_fun/tpks,tksc->tpc/dot_general | solution.py:124
  248.0 3.6 all-to-all-start.10
  251.7 0.6 sine_multiply_fusion.1
  252.3 3.9 convert_bitcast_fusion.6
  256.2 9.4 %bitcast_convert_fusion = bf16[8,672,256]{2,1,0:T(8,128)(2,1)} fusion(bf16[8,31,31,256]{3,1,0,2:T(8,128)(2,1)S(1)} %convert_bitcast_fusion.6, s32[8,31,31]{1,2,0:T(8,128)S(1)} %copy.114), kind=kOutput, calls=%fused_computation.97 | convolution fusion | flops 2651706624 | bytes 6719520 | tf_op jit(solution)/shard_map/cond/branch_1_fun/tpks,tksc->tpc/dot_general | solution.py:124
  265.7 47.7 %all-to-all-done.10 = bf16[8,672,256]{2,1,0:T(8,128)(2,1)S(1)} async-done(((bf16[8,672,256]{2,1,0:T(8,128)(2,1)}), bf16[8,672,256]{2,1,0:T(8,128)(2,1)S(1)}, u32[]{:S(2)}, u32[]{:S(2)}) %all-to-all-start.10) | async-done | bytes 2752544 | tf_op jit(solution)/shard_map/cond/branch_1_fun/all_to_all | solution.py:127
  313.4 1.6 copy-done.9
  315.0 3.9 all-to-all-start.11
  318.9 7.1 %fusion.197 = bf16[8,31,31,256]{3,2,0,1:T(8,128)(2,1)} fusion(s32[8,31,31]{2,0,1:T(8,128)S(1)} %copy.115, bf16[8,672,256]{2,1,0:T(8,128)(2,1)} %copy-done.9), kind=kOutput, calls=%fused_computation.111.clone.1 | convolution fusion | flops 2652298496 | bytes 6719520 | tf_op jit(solution)/shard_map/cond/branch_1_fun/tpks,tpc->tksc/dot_general | solution.py:128
  326.0 13.7 %fusion.64 = bf16[31,8,31,256]{3,2,1,0:T(8,128)(2,1)} fusion(bf16[31,256,1024]{2,1,0:T(8,128)(2,1)} %get-tuple-element.73, bf16[8,31,31,1024]{3,2,1,0:T(8,128)(2,1)} %all-gather.11.cloned.1.call-done), kind=kOutput, calls=%fused_computation.68 | convolution fusion | flops 4030726144 | bytes 35934208 | tf_op jit(solution)/shard_map/cond/branch_1_fun/nksd,kcd->nksc/dot_general | solution.py:170
  339.7 12.9 %all-gather.9.cloned.1.call-done = bf16[8,31,31,1024]{3,2,1,0:T(8,128)(2,1)} async-done(((bf16[8,31,31,256]{3,2,1,0:T(8,128)(2,1)}), bf16[8,31,31,1024]{3,2,1,0:T(8,128)(2,1)}) %all-gather.9.cloned.1.call-update) | async-done | bytes 15745040 | tf_op jit(solution)/shard_map/cond/branch_1_fun/all_gather | solution.py:165
  352.6 13.8 %fusion.66 = bf16[31,8,31,256]{3,2,1,0:T(8,128)(2,1)} fusion(bf16[31,256,1024]{2,1,0:T(8,128)(2,1)} %get-tuple-element.73, bf16[8,31,31,1024]{3,2,1,0:T(8,128)(2,1)} %all-gather.9.cloned.1.call-done), kind=kOutput, calls=%fused_computation.70 | convolution fusion | flops 4030726144 | bytes 35934208 | tf_op jit(solution)/shard_map/cond/branch_1_fun/nksd,kcd->nksc/dot_general | solution.py:170
  366.4 9.5 %bitcast_convert_fusion.2 = bf16[8,672,256]{2,1,0:T(8,128)(2,1)} fusion(bf16[31,8,31,256]{3,2,1,0:T(8,128)(2,1)S(1)} %copy-done.26, s32[8,31,31]{2,0,1:T(8,128)S(1)} %copy.115), kind=kOutput, calls=%fused_computation.99 | convolution fusion | flops 2651706624 | bytes 6719520 | tf_op jit(solution)/shard_map/cond/branch_1_fun/tpks,tksc->tpc/dot_general | solution.py:124
  375.9 5.4 all-to-all-done.11
  381.3 4.9 all-to-all-start.9
  386.2 11.0 %bitcast_convert_fusion.4 = bf16[8,672,256]{2,1,0:T(8,128)(2,1)} fusion(bf16[31,8,31,256]{3,2,1,0:T(8,128)(2,1)} %fusion.66, s32[8,31,31]{2,0,1:T(8,128)S(1)} %copy.115), kind=kOutput, calls=%fused_computation.101 | convolution fusion | flops 2651706624 | bytes 6719520 | tf_op jit(solution)/shard_map/cond/branch_1_fun/tpks,tksc->tpc/dot_general | solution.py:124
  397.2 18.6 %fusion.68 = f32[31,256,1024,1]{2,1,3,0:T(8,128)} fusion(bf16[8,31,31,1024]{3,2,1,0:T(8,128)(2,1)} %all-gather.11.cloned.1.call-done, s32[8,31,31]{2,0,1:T(8,128)S(1)} %copy.115, bf16[8,672,256]{2,1,0:T(8,128)(2,1)S(1)} %all-to-all-done.11), kind=kOutput, calls=%fused_computation.72 | convolution fusion | flops 6683024384 | bytes 51034144 | tf_op jit(solution)/shard_map/cond/branch_1_fun/nksc,nksd->kcd/dot_general | solution.py:178
  415.8 32.2 %all-to-all-done.9 = bf16[8,672,256]{2,1,0:T(8,128)(2,1)} async-done(((bf16[8,672,256]{2,1,0:T(8,128)(2,1)}), bf16[8,672,256]{2,1,0:T(8,128)(2,1)}, u32[]{:S(2)}, u32[]{:S(2)}) %all-to-all-start.9) | async-done | bytes 2752544 | tf_op jit(solution)/shard_map/cond/branch_1_fun/all_to_all | solution.py:127
  448.0 3.8 all-to-all-start.7
  451.9 24.3 %fusion.47 = bf16[31,256,1024]{2,1,0:T(8,128)(2,1)} fusion(f32[31,256,1024,1]{2,1,3,0:T(8,128)} %fusion.68, bf16[8,31,31,1024]{3,2,1,0:T(8,128)(2,1)} %all-gather.9.cloned.1.call-done, bf16[8,31,31,256]{3,2,0,1:T(8,128)(2,1)} %fusion.197), kind=kOutput, calls=%fused_computation.49 | convolution fusion | flops 4046979072 | bytes 68440064 | tf_op jit(solution)/shard_map/cond/branch_1_fun/nksc,nksd->kcd/dot_general | solution.py:178
  476.2 6.1 %fusion.56 = bf16[8,31,31,256]{3,1,0,2:T(8,128)(2,1)S(1)} fusion(bf16[8,672,256]{2,1,0:T(8,128)(2,1)} %all-to-all-done.9, s32[8,31,31]{1,2,0:T(8,128)S(1)} %copy-done.16), kind=kOutput, calls=%fused_computation.60 | convolution fusion | flops 2650330368 | bytes 6719520 | tf_op jit(solution)/shard_map/cond/branch_1_fun/tpks,tpc->tksc/dot_general | solution.py:128
  482.3 7.0 %fusion.109 = bf16[31,240,1,256]{3,1,0,2:T(8,128)(2,1)} fusion(f32[240]{0:T(256)S(1)} %copy-done.25, bf16[8,31,31,240]{3,2,1,0:T(8,128)(2,1)S(1)} %copy-done.2, bf16[8,31,31,256]{3,1,0,2:T(8,128)(2,1)S(1)} %fusion.56), kind=kOutput, calls=%fused_computation.126 | convolution fusion | flops 948510720 | bytes 11436736 | tf_op jit(solution)/shard_map/cond/branch_1_fun/tksj,tksc->sjc/dot_general | solution.py:174
  489.2 25.0 %all-to-all-done.7 = bf16[8,672,256]{2,1,0:T(8,128)(2,1)S(1)} async-done(((bf16[8,672,256]{2,1,0:T(8,128)(2,1)}), bf16[8,672,256]{2,1,0:T(8,128)(2,1)S(1)}, u32[]{:S(2)}, u32[]{:S(2)}) %all-to-all-start.7) | async-done | bytes 2752544 | tf_op jit(solution)/shard_map/cond/branch_1_fun/all_to_all | solution.py:127
  514.3 6.0 %fusion.58 = bf16[8,31,31,256]{3,1,0,2:T(8,128)(2,1)S(1)} fusion(bf16[8,672,256]{2,1,0:T(8,128)(2,1)S(1)} %all-to-all-done.7, s32[8,31,31]{1,2,0:T(8,128)S(1)} %copy-done.16), kind=kOutput, calls=%fused_computation.62 | convolution fusion | flops 2650330368 | bytes 6719520 | tf_op jit(solution)/shard_map/cond/branch_1_fun/tpks,tpc->tksc/dot_general | solution.py:128
  520.3 6.9 %fusion.108 = bf16[31,240,1,256]{3,1,0,2:T(8,128)(2,1)} fusion(f32[240]{0:T(256)S(1)} %copy-done.25, bf16[8,31,31,240]{3,2,1,0:T(8,128)(2,1)S(1)} %copy-done.3, bf16[8,31,31,256]{3,1,0,2:T(8,128)(2,1)S(1)} %fusion.58), kind=kOutput, calls=%fused_computation.125 | convolution fusion | flops 948510720 | bytes 11436736 | tf_op jit(solution)/shard_map/cond/branch_1_fun/tksj,tksc->sjc/dot_general | solution.py:174
  527.2 2.8 maximum_bitcast_fusion.1
  530.0 10.1 %copy.160 = bf16[31,240,1,2,256]{4,3,2,1,0:T(2,128)(2,1)S(1)} copy(bf16[31,240,1,2,256]{4,1,0,3,2:T(8,128)(2,1)S(1)} %maximum_bitcast_fusion.1) | data formatting | bytes 15237120 | tf_op jit(solution)/shard_map/conditional
  540.4 3.1 copy-done.8
  (78 shorter events, 2.5 us)
Async XLA Ops:
  10.4 3.5 copy-start.21
  10.4 4.5 copy-start.23
  15.7 1.0 copy-start.13
  16.9 0.7 copy-start.12
  24.5 7.6 %copy-start.14 = (pred[8,31,31]{2,1,0:T(8,128)(4,1)S(1)}, pred[8,31,31]{2,1,0:T(8,128)(4,1)}, u32[]{:S(2)}) copy-start(pred[8,31,31]{2,1,0:T(8,128)(4,1)} %copy-done.13) | copy-start | bytes 23068
  24.5 7.6 %copy-start.18 = (s32[248]{0:T(256)S(1)}, s32[248]{0:T(256)}, u32[]{:S(2)}) copy-start(s32[248]{0:T(256)} %param.11) | copy-start | bytes 2980
  24.5 7.6 %copy-start.22 = (pred[31]{0:T(512)(128)(4,1)S(1)}, pred[31]{0:T(512)(128)(4,1)}, u32[]{:S(2)}) copy-start(pred[31]{0:T(512)(128)(4,1)} %copy-done.21) | copy-start | bytes 97
  24.5 7.6 %copy-start.24 = (s32[31]{0:T(128)S(1)}, s32[31]{0:T(128)}, u32[]{:S(2)}) copy-start(s32[31]{0:T(128)} %copy-done.23) | copy-start | bytes 376
  39.8 0.6 copy-start.19
  40.4 9.6 %copy-start.10 = (s32[8,31,31]{2,1,0:T(8,128)}, s32[8,31,31]{2,1,0:T(8,128)S(1)}, u32[]{:S(2)}) copy-start(s32[8,31,31]{2,1,0:T(8,128)S(1)} %get-tuple-element.68) | copy-start | bytes 92260 | tf_op jit(solution)/shard_map/conditional
  42.4 213.8 %copy-start.15 = (s32[8,31,31]{1,2,0:T(8,128)}, s32[8,31,31]{1,2,0:T(8,128)S(1)}, u32[]{:S(2)}) copy-start(s32[8,31,31]{1,2,0:T(8,128)S(1)} %copy.114) | copy-start | bytes 92260 | tf_op jit(solution)/shard_map/conditional
  42.4 7.6 %copy-start.1 = (bf16[8,31,31,240]{3,2,1,0:T(8,128)(2,1)S(1)}, bf16[8,31,31,240]{3,2,1,0:T(8,128)(2,1)}, u32[]{:S(2)}) copy-start(bf16[8,31,31,240]{3,2,1,0:T(8,128)(2,1)} %get-tuple-element.179) | copy-start | bytes 11070724 | tf_op jit(solution)/shard_map/conditional
  66.2 7.5 %copy-start.17 = (s32[8,961]{1,0:T(8,128)S(1)}, s32[8,961]{1,0:T(8,128)}, u32[]{:S(2)}) copy-start(s32[8,961]{1,0:T(8,128)} %get-tuple-element.70) | copy-start | bytes 92260 | tf_op jit(solution)/shard_map/conditional
  66.2 7.6 %copy-start.11 = (s32[8,31,31]{2,1,0:T(8,128)S(1)}, s32[8,31,31]{2,1,0:T(8,128)}, u32[]{:S(2)}) copy-start(s32[8,31,31]{2,1,0:T(8,128)} %copy-done.10) | copy-start | bytes 92260 | tf_op jit(solution)/shard_map/conditional
  66.2 69.7 %all-to-all-start.8 = ((bf16[8,672,256]{2,1,0:T(8,128)(2,1)}), bf16[8,672,256]{2,1,0:T(8,128)(2,1)S(1)}, u32[]{:S(2)}, u32[]{:S(2)}) async-start(bf16[8,672,256]{2,1,0:T(8,128)(2,1)} %bitcast_convert_fusion.3), calls=%async_computation.8 | async-start | bytes 5505024 | tf_op jit(solution)/shard_map/cond/branch_1_fun/all_to_all | solution.py:127
  73.6 252.4 %all-gather.11.cloned.1.call-start = ((), (), s32[]{:S(2)}) async-start(), calls=%async_computation.15 | async-start | bytes 20316160 | tf_op jit(solution)/shard_map/cond/branch_1_fun/all_gather | solution.py:165
  141.6 211.0 %all-gather.9.cloned.1.call-start = ((), (), s32[]{:S(2)}) async-start(), calls=%async_computation.14 | async-start | bytes 20316160 | tf_op jit(solution)/shard_map/cond/branch_1_fun/all_gather | solution.py:165
  230.4 0.7 copy-start.20
  235.5 3.1 copy-start.6
  248.0 65.4 %all-to-all-start.10 = ((bf16[8,672,256]{2,1,0:T(8,128)(2,1)}), bf16[8,672,256]{2,1,0:T(8,128)(2,1)S(1)}, u32[]{:S(2)}, u32[]{:S(2)}) async-start(bf16[8,672,256]{2,1,0:T(8,128)(2,1)} %bitcast_convert_fusion.1), calls=%async_computation.10 | async-start | bytes 5505024 | tf_op jit(solution)/shard_map/cond/branch_1_fun/all_to_all | solution.py:127
  313.4 1.6 copy-start.9
  315.0 66.3 %all-to-all-start.11 = ((bf16[8,672,256]{2,1,0:T(8,128)(2,1)}), bf16[8,672,256]{2,1,0:T(8,128)(2,1)S(1)}, u32[]{:S(2)}, u32[]{:S(2)}) async-start(bf16[8,672,256]{2,1,0:T(8,128)(2,1)} %bitcast_convert_fusion), calls=%async_computation.11 | async-start | bytes 5505024 | tf_op jit(solution)/shard_map/cond/branch_1_fun/all_to_all | solution.py:127
  352.6 13.8 %copy-start.26 = (bf16[31,8,31,256]{3,2,1,0:T(8,128)(2,1)S(1)}, bf16[31,8,31,256]{3,2,1,0:T(8,128)(2,1)}, u32[]{:S(2)}) copy-start(bf16[31,8,31,256]{3,2,1,0:T(8,128)(2,1)} %fusion.64) | copy-start | bytes 11808772 | tf_op jit(solution)/shard_map/conditional
  381.3 66.7 %all-to-all-start.9 = ((bf16[8,672,256]{2,1,0:T(8,128)(2,1)}), bf16[8,672,256]{2,1,0:T(8,128)(2,1)}, u32[]{:S(2)}, u32[]{:S(2)}) async-start(bf16[8,672,256]{2,1,0:T(8,128)(2,1)} %bitcast_convert_fusion.2), calls=%async_computation.9 | async-start | bytes 5505024 | tf_op jit(solution)/shard_map/cond/branch_1_fun/all_to_all | solution.py:127
  448.0 66.2 %all-to-all-start.7 = ((bf16[8,672,256]{2,1,0:T(8,128)(2,1)}), bf16[8,672,256]{2,1,0:T(8,128)(2,1)S(1)}, u32[]{:S(2)}, u32[]{:S(2)}) async-start(bf16[8,672,256]{2,1,0:T(8,128)(2,1)} %bitcast_convert_fusion.4), calls=%async_computation.7 | async-start | bytes 5505024 | tf_op jit(solution)/shard_map/cond/branch_1_fun/all_to_all | solution.py:127
  451.9 24.3 %copy-start.16 = (s32[8,31,31]{1,2,0:T(8,128)S(1)}, s32[8,31,31]{1,2,0:T(8,128)}, u32[]{:S(2)}) copy-start(s32[8,31,31]{1,2,0:T(8,128)} %copy-done.15) | copy-start | bytes 92260 | tf_op jit(solution)/shard_map/conditional
  476.2 6.1 %copy-start.2 = (bf16[8,31,31,240]{3,2,1,0:T(8,128)(2,1)S(1)}, bf16[8,31,31,240]{3,2,1,0:T(8,128)(2,1)}, u32[]{:S(2)}) copy-start(bf16[8,31,31,240]{3,2,1,0:T(8,128)(2,1)} %get-tuple-element.179) | copy-start | bytes 11070724 | tf_op jit(solution)/shard_map/conditional
  476.2 6.1 %copy-start.25 = (f32[240]{0:T(256)S(1)}, f32[240]{0:T(256)}, u32[]{:S(2)}) copy-start(f32[240]{0:T(256)} %sine_multiply_fusion.1) | copy-start | bytes 2884 | tf_op jit(solution)/shard_map/conditional
  514.3 6.0 %copy-start.3 = (bf16[8,31,31,240]{3,2,1,0:T(8,128)(2,1)S(1)}, bf16[8,31,31,240]{3,2,1,0:T(8,128)(2,1)}, u32[]{:S(2)}) copy-start(bf16[8,31,31,240]{3,2,1,0:T(8,128)(2,1)} %get-tuple-element.179) | copy-start | bytes 11070724 | tf_op jit(solution)/shard_map/conditional
  520.3 7.0 %copy-start.4 = (bf16[31,240,1,256]{3,1,0,2:T(8,128)(2,1)S(1)}, bf16[31,240,1,256]{3,1,0,2:T(8,128)(2,1)}, u32[]{:S(2)}) copy-start(bf16[31,240,1,256]{3,1,0,2:T(8,128)(2,1)} %fusion.109) | copy-start | bytes 11427844 | tf_op jit(solution)/shard_map/conditional
  540.4 3.1 copy-start.8
Sparse Core Ops, SparseCore 0:
  141.7 104.1 all-gather.10
  247.5 105.0 all-gather.8
